TPU v7x, 256 devices: a whole 4x4x8 slice. The times are simulated.
256 devices in a mesh: row: 16 (over x, y), col: 16 (over z, core).
Axes of the slice: x: 4, y: 4, z: 8, core: 2. Of those that a mesh axis runs over, the one named last changes fastest.
Arguments:
- anc_inverse: float32 [10240, 10240], P('row', 'col'), may hold values from -0.0625 to 0.0625
- lower_anc: float32 [10240, 3, 384], P('col', None, 'row'), may hold values from -1.5 to 1.5
- upper_anc: float32 [10240, 3, 384], P('row', None, 'col'), may hold values from -0.75 to 0.75
- lower_edge: float32 [2, 384, 384], replicated, may hold values from -0.3125 to 0.3125
- upper_edge: float32 [2, 384, 384], replicated, may hold values from -0.3125 to 0.3125
- diag_inverse: float32 [3, 384, 384], replicated, may hold values from -6 to 6
- tile_mask: int32 [3, 80, 3], replicated, may hold values 0 or 1
Outputs:
- x_blocks: float32 [10240, 3, 384], P(('row', 'col'))
- y_blocks: float32 [16, 16, 40, 3, 384], P('col', 'row')
- z_blocks: float32 [3, 384, 384], P(None, 'row', 'col')
- cross_blocks: float32 [2, 2, 384, 384], P(None, None, 'row', 'col')
All inputs are finite; a program needn't handle non-finite values.
Results may differ from a plain program's by a relative error of at most 0.0001.
Values sent between devices are 32-bit elements; how exact they have to be, the bound alone decides.
No kernel may reach another device: no remote copies, remote signals or barrier semaphores. Data moves between devices by JAX's collectives and lax.ppermute only.
A program may use at most 128 MiB of HBM per device.

v0:
```python
import jax
import jax.numpy as jnp
from jax import lax
from jax.experimental import pallas as pl
from jax.experimental.pallas import tpu as pltpu
from jax.sharding import PartitionSpec as P

W = 384
BLK = 128
SUPER = 3
EDGES = 2
XS, YS, ZS, CS = 4, 4, 8, 2

precise = lax.Precision.HIGHEST


def contract(left, right, ldim, rdim):
    return lax.dot_general(
        left, right, (((ldim,), (rdim,)), ((), ())), precision=precise, preferred_element_type=jnp.float32
    )


def to_row(value, dx, dy):
    pairs = [
        (x * YS + y, ((x + dx) % XS) * YS + (y + dy) % YS) for x in range(XS) for y in range(YS)
    ]
    return lax.ppermute(value, "row", pairs)


def to_col(value, dz, dc):
    pairs = [(z * CS + c, ((z + dz) % ZS) * CS + (c ^ dc)) for z in range(ZS) for c in range(CS)]
    return lax.ppermute(value, "col", pairs)


GATHER_STEPS = ((0,), (1, -1), (2, -2), (3, -3), (4,))


def gather_col(value):
    up, down = [value], [value]
    for _ in range(3):
        up.append(to_col(up[-1], 1, 0))
        down.append(to_col(down[-1], -1, 0))
    far = jnp.concatenate([to_col(up[3][:40], 1, 0), to_col(down[3][40:], -1, 0)], axis=0)
    blocks = [value[None]]
    for t in range(1, 4):
        blocks.append(jnp.stack([up[t], down[t]]))
    blocks.append(far[None])
    return blocks, [to_col(block, 0, 1) for block in blocks]


def scatter_col(mine, both):
    q = [mine[d] + both[d] for d in range(ZS)]
    q[0], q[1], q[2], q[6], q[7] = lax.optimization_barrier((q[0], q[1], q[2], q[6], q[7]))
    cut = 40
    u = to_col(q[4][:cut], 1, 0)
    d = to_col(q[4][cut:], -1, 0)
    for left in range(3, 0, -1):
        if left == 3:
            u = jnp.concatenate([q[3][:cut] + u, q[3][cut:]], axis=0)
            d = jnp.concatenate([q[5][:cut], q[5][cut:] + d], axis=0)
        else:
            u, d = q[left] + u, q[ZS - left] + d
        u, d = to_col(u, 1, 0), to_col(d, -1, 0)
    return q[0] + u + d


def scatter_row(parts, gate):
    parts = parts.reshape(XS, YS, *parts.shape[1:])
    lines = [to_row(parts[d], d, 0) for d in range(1, XS)]
    lines = parts[0] + sum(lines)
    ends = [to_row(lines[d], 0, d) for d in range(1, YS)]
    ends, gate = lax.optimization_barrier((ends, gate))
    return [lines[0], *ends], gate


def halves(value):
    high = value.astype(jnp.bfloat16)
    low = (value - high.astype(jnp.float32)).astype(jnp.bfloat16)
    return high, low


def dot3(left, right, ldim, rdim):
    def one(a, b):
        return lax.dot_general(a, b, (((ldim,), (rdim,)), ((), ())), preferred_element_type=jnp.float32)

    return one(left[0], right[0]) + (one(left[0], right[1]) + one(left[1], right[0]))


def started(source, target, semaphore):
    copy = pltpu.make_async_copy(source, target, semaphore)
    copy.start()
    return copy


def rows_kernel(owner_ref, *refs):
    count = 2 * len(GATHER_STEPS)
    pieces = refs[:count]
    edge_hbm, anc_hbm, upper_hbm, out_hbm, edge_ref, anc_ref, upper_ref, out_ref, arrived, piece_in, gone = refs[count:]
    part = pieces[0].shape[1] // SUPER
    anc_copy = started(anc_hbm, anc_ref, arrived.at[0])
    edge_copy = started(edge_hbm, edge_ref, arrived.at[1])
    piece_copies = [[] for _ in range(SUPER)]
    for s in range(SUPER):
        for dc in range(CS):
            for block, steps in enumerate(GATHER_STEPS):
                ref = pieces[dc * len(GATHER_STEPS) + block]
                for k, dz in enumerate(steps):
                    start = pl.multiple_of(owner_ref[dc * ZS + dz % ZS] * part, 8)
                    piece_copies[s].append(
                        started(
                            ref.at[k, pl.ds(s * part, part), :],
                            upper_ref.at[s, pl.ds(start, part), :],
                            piece_in.at[s, len(piece_copies[s])],
                        )
                    )
    anc_copy.wait()
    anc = halves(anc_ref[...])
    leaving = []
    for s in range(SUPER):
        for copy in piece_copies[s]:
            copy.wait()
        if s == 1:
            edge_copy.wait()
        if s > 0:
            upper_ref[s] = upper_ref[s] - dot3(halves(edge_ref[s - 1]), prev, 1, 0)
        leaving.append(started(upper_ref.at[s], upper_hbm.at[s], gone.at[0, s]))
        if s < EDGES:
            prev = halves(upper_ref[s])

    def leave(s):
        start = pl.multiple_of(s * W, BLK)
        return pltpu.make_async_copy(out_ref.at[s], out_hbm.at[:, pl.ds(start, W)], gone.at[1, s])

    @pl.loop(0, SUPER)
    def _(s):
        out_ref[s] = -jnp.transpose(dot3(halves(upper_ref[s]), anc, 1, 0))
        leave(s).start()

    for copy in leaving:
        copy.wait()
    for s in range(SUPER):
        leave(s).wait()


def cols_kernel(owner_ref, lower_hbm, edge_hbm, anc_hbm, mine_hbm, other_hbm, edge_ref, anc_ref, lower_ref, full_ref, arrived, gone):
    _, group, part, depth = lower_ref.shape
    anc_copy = started(anc_hbm, anc_ref, arrived.at[0])
    lower_copies = [
        started(lower_hbm.at[:, pl.ds(s * part, part), :], lower_ref.at[s], arrived.at[2 + s])
        for s in range(SUPER)
    ]
    edge_copy = started(edge_hbm, edge_ref, arrived.at[1])
    anc_copy.wait()
    anc = halves(anc_ref[...])
    for s in range(SUPER):
        lower_copies[s].wait()
        lower = lower_ref[s].reshape(group * part, depth)
        if s == 1:
            edge_copy.wait()
        if s > 0:
            lower = lower - dot3(halves(jnp.transpose(edge_ref[s - 1])), prev, 1, 0)
            lower_ref[s] = lower.reshape(lower_ref.shape[1:])
        if s < EDGES:
            prev = halves(lower)

    def leave(s):
        copies = []
        for dc, ref in enumerate((mine_hbm, other_hbm)):
            for dz in range(ZS):
                start = pl.multiple_of(owner_ref[dc * ZS + dz] * part, 8)
                end = pl.multiple_of(s * part, 8)
                copies.append(
                    pltpu.make_async_copy(
                        full_ref.at[s, pl.ds(start, part), :],
                        ref.at[dz, pl.ds(end, part), :],
                        gone.at[s, dc * ZS + dz],
                    )
                )
        return copies

    @pl.loop(0, SUPER)
    def _(s):
        lower = halves(lower_ref[s].reshape(group * part, depth))
        full_ref[s] = -dot3(lower, anc, 1, 1)
        for copy in leave(s):
            copy.start()

    for s in range(SUPER):
        for copy in leave(s):
            copy.wait()


def masked(mask_ref, ref, s, first_block, first_row):
    _, part, depth = ref.shape
    tile = (first_row + lax.broadcasted_iota(jnp.int32, (part, BLK), 0)) // BLK
    wide = []
    for b in range(depth // BLK):
        pattern = jnp.zeros((part, BLK), jnp.float32)
        for t in range(W // BLK):
            entry = mask_ref[s, t, first_block + b].astype(jnp.float32)
            pattern = jnp.where(tile == t, entry, pattern)
        wide.append(ref[s, :, b * BLK : (b + 1) * BLK] * pattern)
    return jnp.concatenate(wide, axis=1)


def enter_upper_kernel(place_ref, mask_ref, upper_ref, mine_ref):
    _, part, depth = upper_ref.shape
    blocks = depth // BLK
    for s in range(SUPER):
        value = masked(mask_ref, upper_ref, s, place_ref[0] * blocks, place_ref[1] * part)
        mine_ref[s * part : (s + 1) * part, :] = value


def enter_lower_kernel(place_ref, mask_ref, _, lower_ref, send_hbm, held_ref, gone):
    _, part, depth = lower_ref.shape
    blocks = depth // BLK
    for s in range(SUPER):
        value = masked(mask_ref, lower_ref, s, place_ref[1] * blocks, place_ref[0] * part)
        held_ref[s * part : (s + 1) * part, :] = value
    copies = [started(held_ref, send_hbm.at[k], gone.at[k]) for k in range(16)]
    for copy in copies:
        copy.wait()


def fold_kernel(_, got_hbm, out_ref, got_ref, arrived):
    group, half = got_ref.shape[0], got_ref.shape[0] // 2
    copies = [
        started(got_hbm.at[pl.ds(k * half, half)], got_ref.at[pl.ds(k * half, half)], arrived.at[k])
        for k in range(2)
    ]
    for s in range(SUPER):
        if s == 0:
            copies[0].wait()
        total = got_ref[0, :, s * W : (s + 1) * W]
        for k in range(1, group):
            if s == 0 and k == half:
                copies[1].wait()
            total = total + got_ref[k, :, s * W : (s + 1) * W]
        out_ref[s] = total


def couple_kernel(owner_ref, upper_ref, cols_ref, out_ref, sent_ref, tall_ref):
    group, wide, _ = out_ref.shape
    sent_ref[...] = jnp.transpose(cols_ref[...]).reshape(sent_ref.shape)
    part = wide // SUPER
    cols = halves(cols_ref[...])
    for s in range(SUPER):
        tall_ref[...] = dot3(halves(upper_ref[s]), cols, 1, 1)
        for k in range(group):
            start = pl.multiple_of(owner_ref[k] * part, 8)
            out_ref[k, s * part : (s + 1) * part, :] = tall_ref[pl.ds(start, part), :]


def ends_kernel(place_ref, _, lower_ref, upper_ref, diag_ref, out_ref):
    part = out_ref.shape[1]
    mine = pl.ds(pl.multiple_of(place_ref[0] * part, 8), part)
    lower = [halves(lower_ref[s]) for s in range(EDGES)]
    diag = [halves(diag_ref[s]) for s in range(EDGES)]
    upper = [halves(upper_ref[s]) for s in range(EDGES - 1)]

    def times(value, matrix):
        return dot3(halves(value), matrix, 1, 0)

    corner, left, above = [diag_ref[0, mine, :]], [], []
    for s in range(1, SUPER):
        moved = upper_ref[s - 1, mine, :]
        total = times(moved, diag[s - 1])
        for back in range(s - 1, 0, -1):
            moved = times(moved, upper[back - 1])
            term = times(moved, diag[back - 1])
            for edge in range(back - 1, s - 1):
                term = times(term, lower[edge])
            total = total + term
        left.append(times(corner[-1], lower[s - 1]))
        above.append(total)
        corner.append(diag_ref[s, mine, :] + times(total, lower[s - 1]))
    full = jnp.concatenate(corner + left + above, axis=0)
    row = lax.broadcasted_iota(jnp.int32, (W, part), 0)
    col = lax.broadcasted_iota(jnp.int32, (W, part), 1)
    pick = jnp.where(row == col + place_ref[1] * part, 1.0, 0.0).astype(jnp.bfloat16)
    high, rest = halves(full)
    low = (full - high.astype(jnp.float32) - rest.astype(jnp.float32)).astype(jnp.bfloat16)
    out = jnp.zeros(out_ref.shape, jnp.float32)
    for value in (low, rest, high):
        out = out + jnp.dot(value, pick, preferred_element_type=jnp.float32)
    out_ref[...] = out


def tiles_kernel(_, a_ref, b_ref, c_ref, d_ref, ends_ref, got_ref, corner_ref, cross_ref, x_ref):
    part = ends_ref.shape[1]
    total = (a_ref[...] + b_ref[...]) + (c_ref[...] + d_ref[...])

    def tile(s, t):
        return total[s * part : (s + 1) * part, t * part : (t + 1) * part]

    def end(k):
        return ends_ref[k * part : (k + 1) * part, :]

    for s in range(SUPER):
        corner_ref[s] = end(s) - tile(s, s)
    for s in range(EDGES):
        cross_ref[0, s] = -(tile(s, s + 1) + end(SUPER + s))
        cross_ref[1, s] = -(tile(s + 1, s) + end(SUPER + EDGES + s))
    for s in range(SUPER):
        for k in range(got_ref.shape[0]):
            x_ref[s, :, k * part : (k + 1) * part] = got_ref[k, :, s * part : (s + 1) * part]


def call(kernel, outs, inputs, flops, spaces, scratch=()):
    inputs = [
        pltpu.with_memory_space_constraint(value, pltpu.HBM) if space == "h" else value
        for value, space in zip(inputs, spaces)
    ]
    named = {"a": pl.ANY, "s": pltpu.SMEM, "v": pltpu.VMEM, "h": pltpu.HBM}
    specs = [pl.BlockSpec(memory_space=named[space]) for space in spaces]
    return pl.pallas_call(
        kernel,
        out_shape=[
            pltpu.HBM(o, jnp.float32) if space == "h" else jax.ShapeDtypeStruct(o, jnp.float32)
            for o, space in zip(outs, spaces[len(inputs) :])
        ],
        in_specs=specs[: len(inputs)],
        out_specs=specs[len(inputs) :],
        scratch_shapes=list(scratch),
        compiler_params=pltpu.CompilerParams(vmem_limit_bytes=24 * 1024 * 1024),
        cost_estimate=pl.CostEstimate(flops=flops, bytes_accessed=1024, transcendentals=0),
    )(*inputs)


def per_device(anc_inverse, lower_anc, upper_anc, lower_edge, upper_edge, diag_inverse, tile_mask):
    rows_here, cols_here = anc_inverse.shape
    row_index = lax.axis_index("row")
    col_index = lax.axis_index("col")
    z_index, c_index = col_index // CS, col_index % CS
    part = W // 16
    first_row, first_col = row_index * part, col_index * part
    wide = SUPER * part

    place = jnp.stack([row_index, col_index]).astype(jnp.int32)
    mask = jnp.transpose(tile_mask, (0, 2, 1))
    (upper_mine,) = call(
        enter_upper_kernel,
        [(wide, rows_here)],
        [place, mask, jnp.transpose(upper_anc, (1, 2, 0))],
        1000,
        "ssvv",
    )
    (lower_all,) = call(
        enter_lower_kernel,
        [(16, wide, cols_here)],
        [place, mask, upper_mine, jnp.transpose(lower_anc, (1, 2, 0))],
        1000,
        "ssavh",
        [pltpu.VMEM((wide, cols_here), jnp.float32), pltpu.SemaphoreType.DMA((16,))],
    )
    lower_all = lax.all_to_all(lower_all, "row", 0, 0)
    upper_own, upper_sibling = gather_col(upper_mine)

    steps = jnp.arange(ZS, dtype=jnp.int32)
    came = (z_index - steps) % ZS * CS
    goes = (z_index + steps) % ZS * CS
    came = jnp.concatenate([came + c_index, came + 1 - c_index]).astype(jnp.int32)
    goes = jnp.concatenate([goes + c_index, goes + 1 - c_index]).astype(jnp.int32)
    flops = 6 * SUPER * W * rows_here * cols_here + 6 * EDGES * W * W * rows_here

    uppers, rows_part = call(
        rows_kernel,
        [(SUPER, W, rows_here), (cols_here, SUPER * W)],
        [came, *upper_own, *upper_sibling, upper_edge, anc_inverse],
        flops,
        "s" + "h" * (2 * len(GATHER_STEPS)) + "hhhh",
        [
            pltpu.VMEM(upper_edge.shape, jnp.float32),
            pltpu.VMEM(anc_inverse.shape, jnp.float32),
            pltpu.VMEM((SUPER, W, rows_here), jnp.float32),
            pltpu.VMEM((SUPER, cols_here, W), jnp.float32),
            pltpu.SemaphoreType.DMA((2,)),
            pltpu.SemaphoreType.DMA((SUPER, 16)),
            pltpu.SemaphoreType.DMA((2, SUPER)),
        ],
    )
    lower_all, rows_part = lax.optimization_barrier((lower_all, rows_part))
    cols_own, cols_other = call(
        cols_kernel,
        [(ZS, wide, rows_here), (ZS, wide, rows_here)],
        [goes, lower_all, lower_edge, anc_inverse],
        flops,
        "sahhhh",
        [
            pltpu.VMEM(lower_edge.shape, jnp.float32),
            pltpu.VMEM(anc_inverse.shape, jnp.float32),
            pltpu.VMEM((SUPER, 16, part, cols_here), jnp.float32),
            pltpu.VMEM((SUPER, W, rows_here), jnp.float32),
            pltpu.SemaphoreType.DMA((2 + SUPER,)),
            pltpu.SemaphoreType.DMA((SUPER, 16)),
        ],
    )
    cols_sibling = to_col(cols_other, 0, 1)
    rows_part = rows_part.reshape(16, cols_here // 16, SUPER * W)
    rows_got = lax.all_to_all(rows_part, "row", 0, 0)
    (ends,) = call(
        ends_kernel,
        [(7 * part, part)],
        [place, cols_other, lower_edge, upper_edge, diag_inverse],
        100 * flops,
        "savvvv",
    )
    cols_sibling, ends = lax.optimization_barrier((cols_sibling, ends))
    cols_mine = scatter_col(cols_own, cols_sibling)
    across = jnp.arange(16, dtype=jnp.int32)
    across = (row_index // YS + across // YS) % XS * YS + (row_index + across) % YS
    coupled, sent = call(
        couple_kernel,
        [(16, wide, wide), (16, rows_here // 16, wide)],
        [across.astype(jnp.int32), uppers, cols_mine],
        6 * SUPER * W * wide * rows_here,
        "svvvv",
        [pltpu.VMEM((W, wide), jnp.float32)],
    )
    coupled, sent, rows_got = lax.optimization_barrier((coupled, sent, rows_got))
    got = lax.all_to_all(sent, "col", 0, 0)
    sums, got = scatter_row(coupled, got)
    z_blocks, cross_blocks, x_blocks = call(
        tiles_kernel,
        [(SUPER, part, part), (2, EDGES, part, part), (SUPER, rows_here // 16, W)],
        [place, *sums, ends, got],
        0,
        "svvvvvvvvv",
    )
    x_blocks = jnp.transpose(x_blocks, (1, 0, 2))
    (rows_mine,) = call(
        fold_kernel,
        [(SUPER, cols_here // 16, W)],
        [place, rows_got],
        1000,
        "shv",
        [pltpu.VMEM((16, cols_here // 16, SUPER * W), jnp.float32), pltpu.SemaphoreType.DMA((2,))],
    )
    y_blocks = jnp.transpose(rows_mine, (1, 0, 2))[None, None]
    return (x_blocks, y_blocks, z_blocks, cross_blocks)


def solution(mesh):
    return jax.shard_map(
        per_device,
        mesh=mesh,
        in_specs=(
            P("row", "col"),
            P("col", None, "row"),
            P("row", None, "col"),
            P(),
            P(),
            P(),
            P(),
        ),
        out_specs=(
            P(("row", "col"), None, None),
            P("col", "row", None, None, None),
            P(None, "row", "col"),
            P(None, None, "row", "col"),
        ),
        check_vma=False,
    )
```

profile of v0, /device:TPU:1, one launch (start us, length us, event | category | flops | bytes accessed | tf_op | source)
XLA Modules:
  0.0 143.3 jit_solution(3687107630377638569)
XLA Ops:
  0.7 0.9 copy-done.3
  2.3 0.7 shard_map.102._
  3.1 1.0 copy-done.4
  4.0 2.4 %shard_map.104 = f32[16,72,640]{2,1,0:T(8,128)} custom-call(s32[2]{0:T(128)S(1)} %pad_add_fusion.place_ref._, s32[3,3,80]{2,1,0:T(4,128)S(1)} %bitcast.58, f32[72,640]{1,0:T(8,128)S(1)} %shard_map.102._, f32[3,24,640]{2,1,0:T(8,128)S(1)} %bitcast.56), custom_call_target="tpu_custom_call" | custom-call | flops 1000 | bytes 1024 | tf_op jit(solution)/shard_map/pallas_call | solution.py:316
  6.4 7.6 %all-to-all-start = ((f32[16,72,640]{2,1,0:T(8,128)}), f32[16,72,640]{2,1,0:T(8,128)S(1)}, u32[]{:S(2)}, u32[]{:S(2)}) async-start(f32[16,72,640]{2,1,0:T(8,128)} %shard_map.104), calls=%async_computation | async-start | bytes 5898240 | tf_op jit(solution)/shard_map/all_to_all | solution.py:356
  14.1 5.7 %collective-permute-start.1 = (f32[72,640]{1,0:T(8,128)S(1)}, f32[72,640]{1,0:T(8,128)S(1)}, u32[]{:S(2)}, u32[]{:S(2)}) collective-permute-start(f32[72,640]{1,0:T(8,128)S(1)} %shard_map.102._), channel_id=1, source_target_pairs={{0,14},{1,15},{2,0},{3,1},{4,2},{5,3},{6,4},{7,5},{8,6},{9,7},{10,... | collective-permute-start | bytes 552968 | tf_op jit(solution)/shard_map/ppermute | solution.py:32
  19.7 3.0 %collective-permute-done.1 = f32[72,640]{1,0:T(8,128)S(1)} collective-permute-done((f32[72,640]{1,0:T(8,128)S(1)}, f32[72,640]{1,0:T(8,128)S(1)}, u32[]{:S(2)}, u32[]{:S(2)}) %collective-permute-start.1) | collective-permute-done | bytes 184352 | tf_op jit(solution)/shard_map/ppermute | solution.py:32
  22.7 3.4 %collective-permute-start.3 = (f32[72,640]{1,0:T(8,128)S(1)}, f32[72,640]{1,0:T(8,128)}, u32[]{:S(2)}, u32[]{:S(2)}) collective-permute-start(f32[72,640]{1,0:T(8,128)S(1)} %collective-permute-done.1), channel_id=1, source_target_pairs={{0,14},{1,15},{2,0},{3,1},{4,2},{5,3},{6,4},{7,5},{8,6},{9,7},{10,... | collective-permute-start | bytes 552968 | tf_op jit(solution)/shard_map/ppermute | solution.py:32
  26.1 2.5 %collective-permute-done.3 = f32[72,640]{1,0:T(8,128)} collective-permute-done((f32[72,640]{1,0:T(8,128)S(1)}, f32[72,640]{1,0:T(8,128)}, u32[]{:S(2)}, u32[]{:S(2)}) %collective-permute-start.3) | collective-permute-done | bytes 184352 | tf_op jit(solution)/shard_map/ppermute | solution.py:32
  28.6 3.4 %collective-permute-start.5 = (f32[72,640]{1,0:T(8,128)}, f32[72,640]{1,0:T(8,128)S(1)}, u32[]{:S(2)}, u32[]{:S(2)}) collective-permute-start(f32[72,640]{1,0:T(8,128)} %collective-permute-done.3), channel_id=1, source_target_pairs={{0,14},{1,15},{2,0},{3,1},{4,2},{5,3},{6,4},{7,5},{8,6},{9,7},{10,... | collective-permute-start | bytes 552968 | tf_op jit(solution)/shard_map/ppermute | solution.py:32
  32.2 0.9 pad_maximum_fusion.refs_1_
  33.2 3.1 %collective-permute-start.9 = (f32[2,72,640]{2,1,0:T(8,128)S(1)}, f32[2,72,640]{2,1,0:T(8,128)S(1)}, u32[]{:S(2)}, u32[]{:S(2)}) collective-permute-start(f32[2,72,640]{2,1,0:T(8,128)S(1)} %pad_maximum_fusion.refs_1_), channel_id=1, source_target_pairs={{0,1},{1,0},{2,3},{3,2},{4,5},{5,4},{6,7},{7,6},{8,9},{9,8},{10,11... | collective-permute-start | bytes 1105928 | tf_op jit(solution)/shard_map/ppermute | solution.py:32
  36.3 0.9 pad_maximum_fusion.1.refs_2_
  37.4 3.0 %collective-permute-start.7 = (f32[32,640]{1,0:T(8,128)S(1)}, f32[32,640]{1,0:T(8,128)S(1)}, u32[]{:S(2)}, u32[]{:S(2)}) collective-permute-start(f32[32,640]{1,0:T(8,128)S(1)} %slice.157), channel_id=1, source_target_pairs={{0,14},{1,15},{2,0},{3,1},{4,2},{5,3},{6,4},{7,5},{8,6},{9,7},{10,... | collective-permute-start | bytes 245768 | tf_op jit(solution)/shard_map/ppermute | solution.py:32
  40.6 1.8 %collective-permute-start.11 = (f32[2,72,640]{2,1,0:T(8,128)S(1)}, f32[2,72,640]{2,1,0:T(8,128)S(1)}, u32[]{:S(2)}, u32[]{:S(2)}) collective-permute-start(f32[2,72,640]{2,1,0:T(8,128)S(1)} %pad_maximum_fusion.2.refs_3_), channel_id=1, source_target_pairs={{0,1},{1,0},{2,3},{3,2},{4,5},{5,4},{6,7},{7,6},{8,9},{9,8},{10,11... | collective-permute-start | bytes 1105928 | tf_op jit(solution)/shard_map/ppermute | solution.py:32
  42.4 1.8 %collective-permute-start.8 = (f32[1,72,640]{2,1,0:T(8,128)S(1)}, f32[1,72,640]{2,1,0:T(8,128)S(1)}, u32[]{:S(2)}, u32[]{:S(2)}) collective-permute-start(f32[1,72,640]{2,1,0:T(8,128)S(1)} %bitcast.53), channel_id=1, source_target_pairs={{0,1},{1,0},{2,3},{3,2},{4,5},{5,4},{6,7},{7,6},{8,9},{9,8},{10,11... | collective-permute-start | bytes 552968 | tf_op jit(solution)/shard_map/ppermute | solution.py:32
  44.1 1.4 collective-permute-done.6
  45.5 2.8 %collective-permute-start.12 = (f32[1,72,640]{2,1,0:T(8,128)S(1)}, f32[1,72,640]{2,1,0:T(8,128)S(1)}, u32[]{:S(2)}, u32[]{:S(2)}) collective-permute-start(f32[1,72,640]{2,1,0:T(8,128)S(1)} %maximum_bitcast_fusion.refs_4_), channel_id=1, source_target_pairs={{0,1},{1,0},{2,3},{3,2},{4,5},{5,4},{6,7},{7,6},{8,9},{9,8},{10,11... | collective-permute-start | bytes 552968 | tf_op jit(solution)/shard_map/ppermute | solution.py:32
  48.5 0.9 collective-permute-done.12.refs_9_
  50.1 0.7 copy-done.19
  50.8 11.9 %shard_map.103 = (f32[3,384,640]{2,1,0:T(8,128)}, f32[640,1152]{1,0:T(8,128)}) custom-call(s32[16]{0:T(128)S(1)} %pad_add_fusion.1.owner_ref, f32[1,72,640]{2,1,0:T(8,128)} %bitcast.54, f32[2,72,640]{2,1,0:T(8,128)} %copy-done.13, f32[2,72,640]{2,1,0:T(8,128)} %copy-done.14, f32[2,72,640]{2,1,0:T(8,128)} %copy-done.15, f32[1,72,640]{2,1,0:T(8,128)} %copy-done.16, ...), custom_call_target="tpu_custom_call" | custom-call | flops 3963617280 | bytes 1024 | tf_op jit(solution)/shard_map/pallas_call | solution.py:316
  62.7 6.6 %all-to-all-start.1 = ((f32[16,40,1152]{2,1,0:T(8,128)}), f32[16,40,1152]{2,1,0:T(8,128)}, u32[]{:S(2)}, u32[]{:S(2)}) async-start(f32[16,40,1152]{2,1,0:T(8,128)} %bitcast.59), calls=%async_computation.1 | async-start | bytes 5898240 | tf_op jit(solution)/shard_map/all_to_all | solution.py:400
  69.4 10.9 %shard_map.105 = (f32[8,72,640]{2,1,0:T(8,128)}, f32[8,72,640]{2,1,0:T(8,128)}) custom-call(s32[16]{0:T(128)S(1)} %pad_add_fusion.2.owner_ref, f32[16,72,640]{2,1,0:T(8,128)S(1)} %all-to-all-done.lower_hbm, f32[2,384,384]{2,1,0:T(8,128)} %lower_ref.1, f32[640,640]{1,0:T(8,128)} %anc_hbm.1), custom_call_target="tpu_custom_call" | custom-call | flops 3963617280 | bytes 1024 | tf_op jit(solution)/shard_map/pallas_call | solution.py:316
  80.3 0.7 collective-permute-start.13
  81.1 1.4 copy-done.9
  82.4 2.5 %shard_map.106.ends_ref = f32[168,24]{1,0:T(8,128)S(1)} custom-call(s32[2]{0:T(128)S(1)} %pad_add_fusion.place_ref._, f32[8,72,640]{2,1,0:T(8,128)S(1)} %copy-done.9, f32[2,384,384]{2,1,0:T(8,128)S(1)} %copy-done.11, f32[2,384,384]{2,1,0:T(8,128)S(1)} %copy-done.10, f32[3,384,384]{2,1,0:T(8,128)S(1)} %copy-done.8), custom_call_target="tpu_custom_call" | custom-call | flops 396361728000 | bytes 1024 | tf_op jit(solution)/shard_map/pallas_call | solution.py:316
  85.0 1.7 %slice_add_fusion.2 = (f32[1,72,640]{2,1,0:T(8,128)S(1)}, f32[1,72,640]{2,1,0:T(8,128)S(1)}, f32[1,72,640]{2,1,0:T(8,128)S(1)}, f32[72,640]{1,0:T(8,128)S(1)}, f...) fusion(f32[8,72,640]{2,1,0:T(8,128)} %collective-permute-done.13, ...), kind=kLoop, calls=%fused_computation.9 | loop fusion | flops 368640 | bytes 4423680 | tf_op jit(solution)/shard_map/add | solution.py:52
  86.8 1.5 %collective-permute-start.14 = (f32[40,640]{1,0:T(8,128)S(1)}, f32[40,640]{1,0:T(8,128)S(1)}, u32[]{:S(2)}, u32[]{:S(2)}) collective-permute-start(f32[40,640]{1,0:T(8,128)S(1)} %slice_bitcast_fusion.1), channel_id=1, source_target_pairs={{0,2},{1,3},{2,4},{3,5},{4,6},{5,7},{6,8},{7,9},{8,10},{9,11},{10,... | collective-permute-start | bytes 307208 | tf_op jit(solution)/shard_map/ppermute | solution.py:32
  88.4 2.6 %collective-permute-done.18 = f32[32,640]{1,0:T(8,128)S(1)} collective-permute-done((f32[32,640]{1,0:T(8,128)S(1)}, f32[32,640]{1,0:T(8,128)S(1)}, u32[]{:S(2)}, u32[]{:S(2)}) %collective-permute-start.18) | collective-permute-done | bytes 81952 | tf_op jit(solution)/shard_map/ppermute | solution.py:32
  91.0 1.7 %collective-permute-start.19 = (f32[72,640]{1,0:T(8,128)S(1)}, f32[72,640]{1,0:T(8,128)S(1)}, u32[]{:S(2)}, u32[]{:S(2)}) collective-permute-start(f32[72,640]{1,0:T(8,128)S(1)} %pad_maximum_fusion.4), channel_id=1, source_target_pairs={{0,14},{1,15},{2,0},{3,1},{4,2},{5,3},{6,4},{7,5},{8,6},{9,7},{10,... | collective-permute-start | bytes 552968 | tf_op jit(solution)/shard_map/ppermute | solution.py:32
  92.9 3.9 %collective-permute-done.19 = f32[72,640]{1,0:T(8,128)S(1)} collective-permute-done((f32[72,640]{1,0:T(8,128)S(1)}, f32[72,640]{1,0:T(8,128)S(1)}, u32[]{:S(2)}, u32[]{:S(2)}) %collective-permute-start.19) | collective-permute-done | bytes 184352 | tf_op jit(solution)/shard_map/ppermute | solution.py:32
  96.7 3.1 %collective-permute-start.20 = (f32[72,640]{1,0:T(8,128)S(1)}, f32[72,640]{1,0:T(8,128)S(1)}, u32[]{:S(2)}, u32[]{:S(2)}) collective-permute-start(f32[72,640]{1,0:T(8,128)S(1)} %add.171), channel_id=1, source_target_pairs={{0,14},{1,15},{2,0},{3,1},{4,2},{5,3},{6,4},{7,5},{8,6},{9,7},{10,... | collective-permute-start | bytes 552968 | tf_op jit(solution)/shard_map/ppermute | solution.py:32
  99.9 2.4 %collective-permute-done.20 = f32[72,640]{1,0:T(8,128)S(1)} collective-permute-done((f32[72,640]{1,0:T(8,128)S(1)}, f32[72,640]{1,0:T(8,128)S(1)}, u32[]{:S(2)}, u32[]{:S(2)}) %collective-permute-start.20) | collective-permute-done | bytes 184352 | tf_op jit(solution)/shard_map/ppermute | solution.py:32
  102.3 3.8 %collective-permute-start.21 = (f32[72,640]{1,0:T(8,128)S(1)}, f32[72,640]{1,0:T(8,128)S(1)}, u32[]{:S(2)}, u32[]{:S(2)}) collective-permute-start(f32[72,640]{1,0:T(8,128)S(1)} %add.172), channel_id=1, source_target_pairs={{0,14},{1,15},{2,0},{3,1},{4,2},{5,3},{6,4},{7,5},{8,6},{9,7},{10,... | collective-permute-start | bytes 552968 | tf_op jit(solution)/shard_map/ppermute | solution.py:32
  106.1 0.7 add.167
  106.8 1.8 %collective-permute-done.21 = f32[72,640]{1,0:T(8,128)S(1)} collective-permute-done((f32[72,640]{1,0:T(8,128)S(1)}, f32[72,640]{1,0:T(8,128)S(1)}, u32[]{:S(2)}, u32[]{:S(2)}) %collective-permute-start.21) | collective-permute-done | bytes 184352 | tf_op jit(solution)/shard_map/ppermute | solution.py:32
  108.6 4.1 %collective-permute-done.17 = f32[72,640]{1,0:T(8,128)} collective-permute-done((f32[72,640]{1,0:T(8,128)}, f32[72,640]{1,0:T(8,128)}, u32[]{:S(2)}, u32[]{:S(2)}) %collective-permute-start.17) | collective-permute-done | bytes 184352 | tf_op jit(solution)/shard_map/ppermute | solution.py:32
  112.7 1.0 add_add_fusion.cols_ref
  113.7 1.9 %shard_map.107 = (f32[16,72,72]{2,1,0:T(8,128)S(1)}, f32[16,40,72]{2,1,0:T(8,128)S(1)}) custom-call(s32[16]{0:T(128)S(1)} %fusion.2.owner_ref, f32[3,384,640]{2,1,0:T(8,128)S(1)} %copy-done, f32[72,640]{1,0:T(8,128)S(1)} %add_add_fusion.cols_ref), custom_call_target="tpu_custom_call" | custom-call | flops 318504960 | bytes 1024 | tf_op jit(solution)/shard_map/pallas_call | solution.py:316
  115.6 0.7 copy-done.2
  116.4 3.2 %collective-permute-start.23 = (f32[4,72,72]{2,1,0:T(8,128)S(1)}, f32[4,72,72]{2,1,0:T(8,128)S(1)}, u32[]{:S(2)}, u32[]{:S(2)}) collective-permute-start(f32[4,72,72]{2,1,0:T(8,128)S(1)} %get-tuple-element.62), channel_id=1, source_target_pairs={{0,128},{16,144},{32,160},{48,176},{64,192},{80,208},{96,224},{112... | collective-permute-start | bytes 248840 | tf_op jit(solution)/shard_map/ppermute | solution.py:27
  119.5 0.9 collective-permute-start.24
  121.0 7.7 %all-to-all-start.2 = ((f32[16,40,72]{2,1,0:T(8,128)}), f32[16,40,72]{2,1,0:T(8,128)S(1)}, u32[]{:S(2)}, u32[]{:S(2)}) async-start(f32[16,40,72]{2,1,0:T(8,128)} %copy-done.2), calls=%async_computation.2 | async-start | bytes 655360 | tf_op jit(solution)/shard_map/all_to_all | solution.py:421
  128.8 2.5 %collective-permute-start.27 = (f32[72,72]{1,0:T(8,128)S(1)}, f32[72,72]{1,0:T(8,128)S(1)}, u32[]{:S(2)}, u32[]{:S(2)}) collective-permute-start(f32[72,72]{1,0:T(8,128)S(1)} %get-tuple-element.65), channel_id=1, source_target_pairs={{0,48},{16,0},{32,16},{48,32},{64,112},{80,64},{96,80},{112,96},{1... | collective-permute-start | bytes 62216 | tf_op jit(solution)/shard_map/ppermute | solution.py:27
  131.7 0.8 collective-permute-start.25
  132.4 3.2 %shard_map.109 = f32[3,40,384]{2,1,0:T(8,128)} custom-call(s32[2]{0:T(128)S(1)} %pad_add_fusion.place_ref._, f32[16,40,1152]{2,1,0:T(8,128)} %all-to-all-done.1.got_hbm), custom_call_target="tpu_custom_call" | custom-call | flops 1000 | bytes 1024 | tf_op jit(solution)/shard_map/pallas_call | solution.py:316
  136.3 5.4 %all-to-all-done.2.got_ref = f32[16,40,72]{2,1,0:T(8,128)S(1)} async-done(((f32[16,40,72]{2,1,0:T(8,128)}), f32[16,40,72]{2,1,0:T(8,128)S(1)}, u32[]{:S(2)}, u32[]{:S(2)}) %all-to-all-start.2) | async-done | bytes 184352 | tf_op jit(solution)/shard_map/all_to_all | solution.py:421
  141.7 1.6 %shard_map.108 = (f32[3,24,24]{2,1,0:T(8,128)}, f32[2,2,24,24]{3,2,1,0:T(8,128)}, f32[3,40,384]{2,1,0:T(8,128)}) custom-call(s32[2]{0:T(128)S(1)} %pad_add_fusion.place_ref._, f32[72,72]{1,0:T(8,128)S(1)} %get-tuple-element.68.a_ref, f32[72,72]{1,0:T(8,128)S(1)} %collective-permute-done.25.b_ref, f32[72,72]{1,0:T(8,128)S(1)} %collective-permute-done.26.c_ref, ...), custom_call_target="tpu_custom_call" | custom-call | bytes 1024 | tf_op jit(solution)/shard_map/pallas_call | solution.py:316
  (95 shorter events, 4.4 us)
Async XLA Ops:
  3.0 39.3 %copy-start.1 = (f32[72,640]{1,0:T(8,128)}, f32[72,640]{1,0:T(8,128)S(1)}, u32[]{:S(2)}) copy-start(f32[72,640]{1,0:T(8,128)S(1)} %shard_map.102._) | copy-start | bytes 552964
  3.1 1.0 copy-start.4
  6.4 56.2 %all-to-all-start = ((f32[16,72,640]{2,1,0:T(8,128)}), f32[16,72,640]{2,1,0:T(8,128)S(1)}, u32[]{:S(2)}, u32[]{:S(2)}) async-start(f32[16,72,640]{2,1,0:T(8,128)} %shard_map.104), calls=%async_computation | async-start | bytes 5898240 | tf_op jit(solution)/shard_map/all_to_all | solution.py:356
  14.1 8.6 %collective-permute-start.1 = (f32[72,640]{1,0:T(8,128)S(1)}, f32[72,640]{1,0:T(8,128)S(1)}, u32[]{:S(2)}, u32[]{:S(2)}) collective-permute-start(f32[72,640]{1,0:T(8,128)S(1)} %shard_map.102._), channel_id=1, source_target_pairs={{0,14},{1,15},{2,0},{3,1},{4,2},{5,3},{6,4},{7,5},{8,6},{9,7},{10,... | collective-permute-start | bytes 552968 | tf_op jit(solution)/shard_map/ppermute | solution.py:32
  19.7 6.4 %collective-permute-start = (f32[72,640]{1,0:T(8,128)S(1)}, f32[72,640]{1,0:T(8,128)}, u32[]{:S(2)}, u32[]{:S(2)}) collective-permute-start(f32[72,640]{1,0:T(8,128)S(1)} %shard_map.102._), channel_id=1, source_target_pairs={{0,2},{1,3},{2,4},{3,5},{4,6},{5,7},{6,8},{7,9},{8,10},{9,11},{10,... | collective-permute-start | bytes 552968 | tf_op jit(solution)/shard_map/ppermute | solution.py:32
  22.7 5.9 %collective-permute-start.3 = (f32[72,640]{1,0:T(8,128)S(1)}, f32[72,640]{1,0:T(8,128)}, u32[]{:S(2)}, u32[]{:S(2)}) collective-permute-start(f32[72,640]{1,0:T(8,128)S(1)} %collective-permute-done.1), channel_id=1, source_target_pairs={{0,14},{1,15},{2,0},{3,1},{4,2},{5,3},{6,4},{7,5},{8,6},{9,7},{10,... | collective-permute-start | bytes 552968 | tf_op jit(solution)/shard_map/ppermute | solution.py:32
  26.1 6.1 %collective-permute-start.2 = (f32[72,640]{1,0:T(8,128)}, f32[72,640]{1,0:T(8,128)S(1)}, u32[]{:S(2)}, u32[]{:S(2)}) collective-permute-start(f32[72,640]{1,0:T(8,128)} %collective-permute-done), channel_id=1, source_target_pairs={{0,2},{1,3},{2,4},{3,5},{4,6},{5,7},{6,8},{7,9},{8,10},{9,11},{10,... | collective-permute-start | bytes 552968 | tf_op jit(solution)/shard_map/ppermute | solution.py:32
  28.6 8.8 %collective-permute-start.5 = (f32[72,640]{1,0:T(8,128)}, f32[72,640]{1,0:T(8,128)S(1)}, u32[]{:S(2)}, u32[]{:S(2)}) collective-permute-start(f32[72,640]{1,0:T(8,128)} %collective-permute-done.3), channel_id=1, source_target_pairs={{0,14},{1,15},{2,0},{3,1},{4,2},{5,3},{6,4},{7,5},{8,6},{9,7},{10,... | collective-permute-start | bytes 552968 | tf_op jit(solution)/shard_map/ppermute | solution.py:32
  32.2 8.2 %collective-permute-start.4 = (f32[72,640]{1,0:T(8,128)S(1)}, f32[72,640]{1,0:T(8,128)S(1)}, u32[]{:S(2)}, u32[]{:S(2)}) collective-permute-start(f32[72,640]{1,0:T(8,128)S(1)} %collective-permute-done.2), channel_id=1, source_target_pairs={{0,2},{1,3},{2,4},{3,5},{4,6},{5,7},{6,8},{7,9},{8,10},{9,11},{10,... | collective-permute-start | bytes 552968 | tf_op jit(solution)/shard_map/ppermute | solution.py:32
  33.2 16.2 %copy-start.13 = (f32[2,72,640]{2,1,0:T(8,128)}, f32[2,72,640]{2,1,0:T(8,128)S(1)}, u32[]{:S(2)}) copy-start(f32[2,72,640]{2,1,0:T(8,128)S(1)} %pad_maximum_fusion.refs_1_) | copy-start | bytes 1105924
  33.2 15.3 %collective-permute-start.9 = (f32[2,72,640]{2,1,0:T(8,128)S(1)}, f32[2,72,640]{2,1,0:T(8,128)S(1)}, u32[]{:S(2)}, u32[]{:S(2)}) collective-permute-start(f32[2,72,640]{2,1,0:T(8,128)S(1)} %pad_maximum_fusion.refs_1_), channel_id=1, source_target_pairs={{0,1},{1,0},{2,3},{3,2},{4,5},{5,4},{6,7},{7,6},{8,9},{9,8},{10,11... | collective-permute-start | bytes 1105928 | tf_op jit(solution)/shard_map/ppermute | solution.py:32
  37.2 12.2 %copy-start.14 = (f32[2,72,640]{2,1,0:T(8,128)}, f32[2,72,640]{2,1,0:T(8,128)S(1)}, u32[]{:S(2)}) copy-start(f32[2,72,640]{2,1,0:T(8,128)S(1)} %pad_maximum_fusion.1.refs_2_) | copy-start | bytes 1105924
  37.2 11.3 %collective-permute-start.10 = (f32[2,72,640]{2,1,0:T(8,128)S(1)}, f32[2,72,640]{2,1,0:T(8,128)S(1)}, u32[]{:S(2)}, u32[]{:S(2)}) collective-permute-start(f32[2,72,640]{2,1,0:T(8,128)S(1)} %pad_maximum_fusion.1.refs_2_), channel_id=1, source_target_pairs={{0,1},{1,0},{2,3},{3,2},{4,5},{5,4},{6,7},{7,6},{8,9},{9,8},{10,11... | collective-permute-start | bytes 1105928 | tf_op jit(solution)/shard_map/ppermute | solution.py:32
  37.4 5.0 %collective-permute-start.7 = (f32[32,640]{1,0:T(8,128)S(1)}, f32[32,640]{1,0:T(8,128)S(1)}, u32[]{:S(2)}, u32[]{:S(2)}) collective-permute-start(f32[32,640]{1,0:T(8,128)S(1)} %slice.157), channel_id=1, source_target_pairs={{0,14},{1,15},{2,0},{3,1},{4,2},{5,3},{6,4},{7,5},{8,6},{9,7},{10,... | collective-permute-start | bytes 245768 | tf_op jit(solution)/shard_map/ppermute | solution.py:32
  40.4 5.1 %collective-permute-start.6 = (f32[40,640]{1,0:T(8,128)S(1)}, f32[40,640]{1,0:T(8,128)S(1)}, u32[]{:S(2)}, u32[]{:S(2)}) collective-permute-start(f32[40,640]{1,0:T(8,128)S(1)} %slice.156), channel_id=1, source_target_pairs={{0,2},{1,3},{2,4},{3,5},{4,6},{5,7},{6,8},{7,9},{8,10},{9,11},{10,... | collective-permute-start | bytes 307208 | tf_op jit(solution)/shard_map/ppermute | solution.py:32
  40.6 8.8 %copy-start.15 = (f32[2,72,640]{2,1,0:T(8,128)}, f32[2,72,640]{2,1,0:T(8,128)S(1)}, u32[]{:S(2)}) copy-start(f32[2,72,640]{2,1,0:T(8,128)S(1)} %pad_maximum_fusion.2.refs_3_) | copy-start | bytes 1105924
  40.6 8.8 %collective-permute-start.11 = (f32[2,72,640]{2,1,0:T(8,128)S(1)}, f32[2,72,640]{2,1,0:T(8,128)S(1)}, u32[]{:S(2)}, u32[]{:S(2)}) collective-permute-start(f32[2,72,640]{2,1,0:T(8,128)S(1)} %pad_maximum_fusion.2.refs_3_), channel_id=1, source_target_pairs={{0,1},{1,0},{2,3},{3,2},{4,5},{5,4},{6,7},{7,6},{8,9},{9,8},{10,11... | collective-permute-start | bytes 1105928 | tf_op jit(solution)/shard_map/ppermute | solution.py:32
  42.4 6.1 %collective-permute-start.8 = (f32[1,72,640]{2,1,0:T(8,128)S(1)}, f32[1,72,640]{2,1,0:T(8,128)S(1)}, u32[]{:S(2)}, u32[]{:S(2)}) collective-permute-start(f32[1,72,640]{2,1,0:T(8,128)S(1)} %bitcast.53), channel_id=1, source_target_pairs={{0,1},{1,0},{2,3},{3,2},{4,5},{5,4},{6,7},{7,6},{8,9},{9,8},{10,11... | collective-permute-start | bytes 552968 | tf_op jit(solution)/shard_map/ppermute | solution.py:32
  45.5 3.9 %copy-start.16 = (f32[1,72,640]{2,1,0:T(8,128)}, f32[1,72,640]{2,1,0:T(8,128)S(1)}, u32[]{:S(2)}) copy-start(f32[1,72,640]{2,1,0:T(8,128)S(1)} %maximum_bitcast_fusion.refs_4_) | copy-start | bytes 552964
  45.5 3.8 %collective-permute-start.12 = (f32[1,72,640]{2,1,0:T(8,128)S(1)}, f32[1,72,640]{2,1,0:T(8,128)S(1)}, u32[]{:S(2)}, u32[]{:S(2)}) collective-permute-start(f32[1,72,640]{2,1,0:T(8,128)S(1)} %maximum_bitcast_fusion.refs_4_), channel_id=1, source_target_pairs={{0,1},{1,0},{2,3},{3,2},{4,5},{5,4},{6,7},{7,6},{8,9},{9,8},{10,11... | collective-permute-start | bytes 552968 | tf_op jit(solution)/shard_map/ppermute | solution.py:32
  48.5 0.9 copy-start.20
  48.5 0.9 copy-start.17
  48.5 0.9 copy-start.18
  62.7 53.6 %all-to-all-start.1 = ((f32[16,40,1152]{2,1,0:T(8,128)}), f32[16,40,1152]{2,1,0:T(8,128)}, u32[]{:S(2)}, u32[]{:S(2)}) async-start(f32[16,40,1152]{2,1,0:T(8,128)} %bitcast.59), calls=%async_computation.1 | async-start | bytes 5898240 | tf_op jit(solution)/shard_map/all_to_all | solution.py:400
  69.3 11.7 %copy-start.8 = (f32[3,384,384]{2,1,0:T(8,128)S(1)}, f32[3,384,384]{2,1,0:T(8,128)}, u32[]{:S(2)}) copy-start(f32[3,384,384]{2,1,0:T(8,128)} %diag_ref.1) | copy-start | bytes 5308420
  69.4 11.7 %copy-start.10 = (f32[2,384,384]{2,1,0:T(8,128)S(1)}, f32[2,384,384]{2,1,0:T(8,128)}, u32[]{:S(2)}) copy-start(f32[2,384,384]{2,1,0:T(8,128)} %upper_ref.1) | copy-start | bytes 3538948
  69.4 11.7 %copy-start.11 = (f32[2,384,384]{2,1,0:T(8,128)S(1)}, f32[2,384,384]{2,1,0:T(8,128)}, u32[]{:S(2)}) copy-start(f32[2,384,384]{2,1,0:T(8,128)} %lower_ref.1) | copy-start | bytes 3538948
  80.3 4.7 %collective-permute-start.13 = (f32[8,72,640]{2,1,0:T(8,128)}, f32[8,72,640]{2,1,0:T(8,128)}, u32[]{:S(2)}, u32[]{:S(2)}) collective-permute-start(f32[8,72,640]{2,1,0:T(8,128)} %get-tuple-element.33._), channel_id=1, source_target_pairs={{0,1},{1,0},{2,3},{3,2},{4,5},{5,4},{6,7},{7,6},{8,9},{9,8},{10,11... | collective-permute-start | bytes 4423688 | tf_op jit(solution)/shard_map/ppermute | solution.py:32
  81.1 1.4 copy-start.9
  82.4 2.6 %copy-start.12 = (f32[8,72,640]{2,1,0:T(8,128)S(1)}, f32[8,72,640]{2,1,0:T(8,128)}, u32[]{:S(2)}) copy-start(f32[8,72,640]{2,1,0:T(8,128)} %get-tuple-element.32) | copy-start | bytes 4423684
  85.0 1.7 %copy-start.5 = (f32[168,24]{1,0:T(8,128)}, f32[168,24]{1,0:T(8,128)S(1)}, u32[]{:S(2)}) copy-start(f32[168,24]{1,0:T(8,128)S(1)} %shard_map.106.ends_ref) | copy-start | bytes 48388
  86.7 4.2 %collective-permute-start.18 = (f32[32,640]{1,0:T(8,128)S(1)}, f32[32,640]{1,0:T(8,128)S(1)}, u32[]{:S(2)}, u32[]{:S(2)}) collective-permute-start(f32[32,640]{1,0:T(8,128)S(1)} %slice_bitcast_fusion.3), channel_id=1, source_target_pairs={{0,14},{1,15},{2,0},{3,1},{4,2},{5,3},{6,4},{7,5},{8,6},{9,7},{10,... | collective-permute-start | bytes 245768 | tf_op jit(solution)/shard_map/ppermute | solution.py:32
  86.8 5.9 %collective-permute-start.14 = (f32[40,640]{1,0:T(8,128)S(1)}, f32[40,640]{1,0:T(8,128)S(1)}, u32[]{:S(2)}, u32[]{:S(2)}) collective-permute-start(f32[40,640]{1,0:T(8,128)S(1)} %slice_bitcast_fusion.1), channel_id=1, source_target_pairs={{0,2},{1,3},{2,4},{3,5},{4,6},{5,7},{6,8},{7,9},{8,10},{9,11},{10,... | collective-permute-start | bytes 307208 | tf_op jit(solution)/shard_map/ppermute | solution.py:32
  91.0 5.8 %collective-permute-start.19 = (f32[72,640]{1,0:T(8,128)S(1)}, f32[72,640]{1,0:T(8,128)S(1)}, u32[]{:S(2)}, u32[]{:S(2)}) collective-permute-start(f32[72,640]{1,0:T(8,128)S(1)} %pad_maximum_fusion.4), channel_id=1, source_target_pairs={{0,14},{1,15},{2,0},{3,1},{4,2},{5,3},{6,4},{7,5},{8,6},{9,7},{10,... | collective-permute-start | bytes 552968 | tf_op jit(solution)/shard_map/ppermute | solution.py:32
  92.7 21.0 %copy-start = (f32[3,384,640]{2,1,0:T(8,128)S(1)}, f32[3,384,640]{2,1,0:T(8,128)}, u32[]{:S(2)}) copy-start(f32[3,384,640]{2,1,0:T(8,128)} %get-tuple-element.29.upper_ref) | copy-start | bytes 8847364
  92.8 7.0 %collective-permute-start.15 = (f32[72,640]{1,0:T(8,128)S(1)}, f32[72,640]{1,0:T(8,128)S(1)}, u32[]{:S(2)}, u32[]{:S(2)}) collective-permute-start(f32[72,640]{1,0:T(8,128)S(1)} %pad_maximum_fusion.3), channel_id=1, source_target_pairs={{0,2},{1,3},{2,4},{3,5},{4,6},{5,7},{6,8},{7,9},{8,10},{9,11},{10,... | collective-permute-start | bytes 552968 | tf_op jit(solution)/shard_map/ppermute | solution.py:32
  96.7 5.5 %collective-permute-start.20 = (f32[72,640]{1,0:T(8,128)S(1)}, f32[72,640]{1,0:T(8,128)S(1)}, u32[]{:S(2)}, u32[]{:S(2)}) collective-permute-start(f32[72,640]{1,0:T(8,128)S(1)} %add.171), channel_id=1, source_target_pairs={{0,14},{1,15},{2,0},{3,1},{4,2},{5,3},{6,4},{7,5},{8,6},{9,7},{10,... | collective-permute-start | bytes 552968 | tf_op jit(solution)/shard_map/ppermute | solution.py:32
  99.8 6.3 %collective-permute-start.16 = (f32[72,640]{1,0:T(8,128)S(1)}, f32[72,640]{1,0:T(8,128)S(1)}, u32[]{:S(2)}, u32[]{:S(2)}) collective-permute-start(f32[72,640]{1,0:T(8,128)S(1)} %add.166), channel_id=1, source_target_pairs={{0,2},{1,3},{2,4},{3,5},{4,6},{5,7},{6,8},{7,9},{8,10},{9,11},{10,... | collective-permute-start | bytes 552968 | tf_op jit(solution)/shard_map/ppermute | solution.py:32
  102.3 6.3 %collective-permute-start.21 = (f32[72,640]{1,0:T(8,128)S(1)}, f32[72,640]{1,0:T(8,128)S(1)}, u32[]{:S(2)}, u32[]{:S(2)}) collective-permute-start(f32[72,640]{1,0:T(8,128)S(1)} %add.172), channel_id=1, source_target_pairs={{0,14},{1,15},{2,0},{3,1},{4,2},{5,3},{6,4},{7,5},{8,6},{9,7},{10,... | collective-permute-start | bytes 552968 | tf_op jit(solution)/shard_map/ppermute | solution.py:32
  106.8 5.9 %collective-permute-start.17 = (f32[72,640]{1,0:T(8,128)}, f32[72,640]{1,0:T(8,128)}, u32[]{:S(2)}, u32[]{:S(2)}) collective-permute-start(f32[72,640]{1,0:T(8,128)} %add.167), channel_id=1, source_target_pairs={{0,2},{1,3},{2,4},{3,5},{4,6},{5,7},{6,8},{7,9},{8,10},{9,11},{10,... | collective-permute-start | bytes 552968 | tf_op jit(solution)/shard_map/ppermute | solution.py:32
  116.4 12.3 %collective-permute-start.23 = (f32[4,72,72]{2,1,0:T(8,128)S(1)}, f32[4,72,72]{2,1,0:T(8,128)S(1)}, u32[]{:S(2)}, u32[]{:S(2)}) collective-permute-start(f32[4,72,72]{2,1,0:T(8,128)S(1)} %get-tuple-element.62), channel_id=1, source_target_pairs={{0,128},{16,144},{32,160},{48,176},{64,192},{80,208},{96,224},{112... | collective-permute-start | bytes 248840 | tf_op jit(solution)/shard_map/ppermute | solution.py:27
  119.5 9.1 %collective-permute-start.24 = (f32[4,72,72]{2,1,0:T(8,128)S(1)}, f32[4,72,72]{2,1,0:T(8,128)S(1)}, u32[]{:S(2)}, u32[]{:S(2)}) collective-permute-start(f32[4,72,72]{2,1,0:T(8,128)S(1)} %get-tuple-element.63), channel_id=1, source_target_pairs={{0,192},{16,208},{32,224},{48,240},{64,0},{80,16},{96,32},{112,48}... | collective-permute-start | bytes 248840 | tf_op jit(solution)/shard_map/ppermute | solution.py:27
  120.4 8.3 %collective-permute-start.22 = (f32[4,72,72]{2,1,0:T(8,128)S(1)}, f32[4,72,72]{2,1,0:T(8,128)S(1)}, u32[]{:S(2)}, u32[]{:S(2)}) collective-permute-start(f32[4,72,72]{2,1,0:T(8,128)S(1)} %get-tuple-element.64), channel_id=1, source_target_pairs={{0,64},{16,80},{32,96},{48,112},{64,128},{80,144},{96,160},{112,17... | collective-permute-start | bytes 248840 | tf_op jit(solution)/shard_map/ppermute | solution.py:27
  121.0 20.7 %all-to-all-start.2 = ((f32[16,40,72]{2,1,0:T(8,128)}), f32[16,40,72]{2,1,0:T(8,128)S(1)}, u32[]{:S(2)}, u32[]{:S(2)}) async-start(f32[16,40,72]{2,1,0:T(8,128)} %copy-done.2), calls=%async_computation.2 | async-start | bytes 655360 | tf_op jit(solution)/shard_map/all_to_all | solution.py:421
  128.8 13.0 %copy-start.6 = (f32[168,24]{1,0:T(8,128)S(1)}, f32[168,24]{1,0:T(8,128)}, u32[]{:S(2)}) copy-start(f32[168,24]{1,0:T(8,128)} %copy-done.5) | copy-start | bytes 48388
  128.8 6.8 %collective-permute-start.27 = (f32[72,72]{1,0:T(8,128)S(1)}, f32[72,72]{1,0:T(8,128)S(1)}, u32[]{:S(2)}, u32[]{:S(2)}) collective-permute-start(f32[72,72]{1,0:T(8,128)S(1)} %get-tuple-element.65), channel_id=1, source_target_pairs={{0,48},{16,0},{32,16},{48,32},{64,112},{80,64},{96,80},{112,96},{1... | collective-permute-start | bytes 62216 | tf_op jit(solution)/shard_map/ppermute | solution.py:27
  131.3 4.6 %collective-permute-start.26 = (f32[72,72]{1,0:T(8,128)S(1)}, f32[72,72]{1,0:T(8,128)S(1)}, u32[]{:S(2)}, u32[]{:S(2)}) collective-permute-start(f32[72,72]{1,0:T(8,128)S(1)} %get-tuple-element.66), channel_id=1, source_target_pairs={{0,32},{16,48},{32,0},{48,16},{64,96},{80,112},{96,64},{112,80},{1... | collective-permute-start | bytes 62216 | tf_op jit(solution)/shard_map/ppermute | solution.py:27
  131.7 4.6 %collective-permute-start.25 = (f32[72,72]{1,0:T(8,128)S(1)}, f32[72,72]{1,0:T(8,128)S(1)}, u32[]{:S(2)}, u32[]{:S(2)}) collective-permute-start(f32[72,72]{1,0:T(8,128)S(1)} %get-tuple-element.67), channel_id=1, source_target_pairs={{0,16},{16,32},{32,48},{48,0},{64,80},{80,96},{96,112},{112,64},{1... | collective-permute-start | bytes 62216 | tf_op jit(solution)/shard_map/ppermute | solution.py:27
  (5 other events, 3.7 us)
where the time goes:
time: 144 us; the launch traced here: 143 us
  starting transfers between devices  66.4 us (46%)
  Pallas kernels  35 us (24%)
  waiting for transfers between devices  28.8 us (20%)
  local copies, waits for them, and re-layouts  6.2 us (4%)
  other arithmetic  5.73 us (4%)
    ppermute x22, starting transfers between devices, to_col(): return lax.ppermute(value, 'col', pairs)  36.2 us
    pallas_call x8, Pallas kernels, call(): pl.pallas_call(kernel, out_shape=[pltpu.HBM(o, jnp.float32) if space == '...  35 us
    ppermute x22, waiting for transfers between devices, to_col(): return lax.ppermute(value, 'col', pairs)  22.6 us
    ppermute x6, starting transfers between devices, to_row(): return lax.ppermute(value, 'row', pairs)  8.3 us
    all_to_all x1, starting transfers between devices, per_device(): got = lax.all_to_all(sent, 'col', 0, 0)  7.67 us
    all_to_all x1, starting transfers between devices, per_device(): lower_all = lax.all_to_all(lower_all, 'row', 0, 0)  7.6 us
    all_to_all x1, starting transfers between devices, per_device(): rows_got = lax.all_to_all(rows_part, 'row', 0, 0)  6.65 us
    unnamed x44, local copies, waits for them, and re-layouts  6.11 us
  transfers between devices with their start and end apart: 31, of which 13 were waited for; matrix products, arithmetic and copies ran while one was open for 4% of the time, Pallas kernels for 21%

commit v1 on v0

--- a/solution.py
+++ b/solution.py
@@ -40,7 +40,7 @@
     for _ in range(3):
         up.append(to_col(up[-1], 1, 0))
         down.append(to_col(down[-1], -1, 0))
-    far = jnp.concatenate([to_col(up[3][:40], 1, 0), to_col(down[3][40:], -1, 0)], axis=0)
+    far = to_col(up[3], 1, 0)
     blocks = [value[None]]
     for t in range(1, 4):
         blocks.append(jnp.stack([up[t], down[t]]))
@@ -51,14 +51,9 @@
 def scatter_col(mine, both):
     q = [mine[d] + both[d] for d in range(ZS)]
     q[0], q[1], q[2], q[6], q[7] = lax.optimization_barrier((q[0], q[1], q[2], q[6], q[7]))
-    cut = 40
-    u = to_col(q[4][:cut], 1, 0)
-    d = to_col(q[4][cut:], -1, 0)
+    u, d = q[3] + to_col(q[4], 1, 0), q[5]
     for left in range(3, 0, -1):
-        if left == 3:
-            u = jnp.concatenate([q[3][:cut] + u, q[3][cut:]], axis=0)
-            d = jnp.concatenate([q[5][:cut], q[5][cut:] + d], axis=0)
-        else:
+        if left < 3:
             u, d = q[left] + u, q[ZS - left] + d
         u, d = to_col(u, 1, 0), to_col(d, -1, 0)
     return q[0] + u + d

time: 144 us -> 148 us (1.028)
  waiting for transfers between devices: 28.8 us -> 36.7 us
  starting transfers between devices: 66.4 us -> 62.2 us
    ppermute x22 -> x20, waiting for transfers between devices: 22.6 us -> 30.5 us  [to_col(): return lax.ppermute(value, 'col', pairs)]
    ppermute x22 -> x20, starting transfers between devices: 36.2 us -> 32.2 us  [to_col(): return lax.ppermute(value, 'col', pairs)]
    unnamed x44 -> x42, local copies, waits for them, and re-layouts: 6.11 us -> 5.5 us
  transfers between devices with their start and end apart: 31 -> 29, of which waited for: 13 -> 13; matrix products, arithmetic and copies ran while one was open for 4% -> 4% of each run, Pallas kernels for 21% -> 21%
where the time goes in v1:
time: 148 us; the launch traced here: 147 us
  starting transfers between devices  62.2 us (42%)
  waiting for transfers between devices  36.7 us (25%)
  Pallas kernels  35.1 us (24%)
  other arithmetic  6.54 us (4%)
  local copies, waits for them, and re-layouts  5.54 us (4%)
    pallas_call x8, Pallas kernels, call(): pl.pallas_call(kernel, out_shape=[pltpu.HBM(o, jnp.float32) if space == '...  35.1 us
    ppermute x20, starting transfers between devices, to_col(): return lax.ppermute(value, 'col', pairs)  32.2 us
    ppermute x20, waiting for transfers between devices, to_col(): return lax.ppermute(value, 'col', pairs)  30.5 us
    all_to_all x1, starting transfers between devices, per_device(): got = lax.all_to_all(sent, 'col', 0, 0)  8.02 us
    ppermute x6, starting transfers between devices, to_row(): return lax.ppermute(value, 'row', pairs)  7.71 us
    all_to_all x1, starting transfers between devices, per_device(): lower_all = lax.all_to_all(lower_all, 'row', 0, 0)  7.6 us
    all_to_all x1, starting transfers between devices, per_device(): rows_got = lax.all_to_all(rows_part, 'row', 0, 0)  6.63 us
    unnamed x42, local copies, waits for them, and re-layouts  5.5 us
  transfers between devices with their start and end apart: 29, of which 13 were waited for; matrix products, arithmetic and copies ran while one was open for 4% of the time, Pallas kernels for 21%

profile of v1, /device:TPU:1, one launch (start us, length us, event | category | flops | bytes accessed | tf_op | source)
XLA Modules:
  0.0 147.0 jit_solution(6190784184150080597)
XLA Ops:
  0.7 0.9 copy-done.3
  1.6 0.7 copy-done.7
  2.3 0.7 shard_map.102._
  3.1 1.0 copy-done.4
  4.0 2.4 %shard_map.104 = f32[16,72,640]{2,1,0:T(8,128)} custom-call(s32[2]{0:T(128)S(1)} %pad_add_fusion.place_ref._, s32[3,3,80]{2,1,0:T(4,128)S(1)} %bitcast.47, f32[72,640]{1,0:T(8,128)S(1)} %shard_map.102._, f32[3,24,640]{2,1,0:T(8,128)S(1)} %bitcast.45), custom_call_target="tpu_custom_call" | custom-call | flops 1000 | bytes 1024 | tf_op jit(solution)/shard_map/pallas_call | solution.py:311
  6.5 7.6 %all-to-all-start = ((f32[16,72,640]{2,1,0:T(8,128)}), f32[16,72,640]{2,1,0:T(8,128)S(1)}, u32[]{:S(2)}, u32[]{:S(2)}) async-start(f32[16,72,640]{2,1,0:T(8,128)} %shard_map.104), calls=%async_computation | async-start | bytes 5898240 | tf_op jit(solution)/shard_map/all_to_all | solution.py:351
  14.1 5.7 %collective-permute-start.1 = (f32[72,640]{1,0:T(8,128)S(1)}, f32[72,640]{1,0:T(8,128)S(1)}, u32[]{:S(2)}, u32[]{:S(2)}) collective-permute-start(f32[72,640]{1,0:T(8,128)S(1)} %shard_map.102._), channel_id=1, source_target_pairs={{0,14},{1,15},{2,0},{3,1},{4,2},{5,3},{6,4},{7,5},{8,6},{9,7},{10,... | collective-permute-start | bytes 552968 | tf_op jit(solution)/shard_map/ppermute | solution.py:32
  19.7 3.0 %collective-permute-done.1 = f32[72,640]{1,0:T(8,128)S(1)} collective-permute-done((f32[72,640]{1,0:T(8,128)S(1)}, f32[72,640]{1,0:T(8,128)S(1)}, u32[]{:S(2)}, u32[]{:S(2)}) %collective-permute-start.1) | collective-permute-done | bytes 184352 | tf_op jit(solution)/shard_map/ppermute | solution.py:32
  22.7 3.4 %collective-permute-start.3 = (f32[72,640]{1,0:T(8,128)S(1)}, f32[72,640]{1,0:T(8,128)S(1)}, u32[]{:S(2)}, u32[]{:S(2)}) collective-permute-start(f32[72,640]{1,0:T(8,128)S(1)} %collective-permute-done.1), channel_id=1, source_target_pairs={{0,14},{1,15},{2,0},{3,1},{4,2},{5,3},{6,4},{7,5},{8,6},{9,7},{10,... | collective-permute-start | bytes 552968 | tf_op jit(solution)/shard_map/ppermute | solution.py:32
  26.1 2.2 %collective-permute-start.7 = (f32[1,72,640]{2,1,0:T(8,128)S(1)}, f32[1,72,640]{2,1,0:T(8,128)}, u32[]{:S(2)}, u32[]{:S(2)}) collective-permute-start(f32[1,72,640]{2,1,0:T(8,128)S(1)} %bitcast.42), channel_id=1, source_target_pairs={{0,1},{1,0},{2,3},{3,2},{4,5},{5,4},{6,7},{7,6},{8,9},{9,8},{10,11... | collective-permute-start | bytes 552968 | tf_op jit(solution)/shard_map/ppermute | solution.py:32
  28.6 3.4 %collective-permute-start.5 = (f32[72,640]{1,0:T(8,128)S(1)}, f32[72,640]{1,0:T(8,128)S(1)}, u32[]{:S(2)}, u32[]{:S(2)}) collective-permute-start(f32[72,640]{1,0:T(8,128)S(1)} %collective-permute-done.3), channel_id=1, source_target_pairs={{0,14},{1,15},{2,0},{3,1},{4,2},{5,3},{6,4},{7,5},{8,6},{9,7},{10,... | collective-permute-start | bytes 552968 | tf_op jit(solution)/shard_map/ppermute | solution.py:32
  32.2 0.9 pad_maximum_fusion.refs_1_
  33.2 3.2 %collective-permute-start.8 = (f32[2,72,640]{2,1,0:T(8,128)S(1)}, f32[2,72,640]{2,1,0:T(8,128)S(1)}, u32[]{:S(2)}, u32[]{:S(2)}) collective-permute-start(f32[2,72,640]{2,1,0:T(8,128)S(1)} %pad_maximum_fusion.refs_1_), channel_id=1, source_target_pairs={{0,1},{1,0},{2,3},{3,2},{4,5},{5,4},{6,7},{7,6},{8,9},{9,8},{10,11... | collective-permute-start | bytes 1105928 | tf_op jit(solution)/shard_map/ppermute | solution.py:32
  36.4 0.9 pad_maximum_fusion.1.refs_2_
  37.5 0.8 collective-permute-done.4
  38.4 4.0 %collective-permute-start.10 = (f32[2,72,640]{2,1,0:T(8,128)S(1)}, f32[2,72,640]{2,1,0:T(8,128)S(1)}, u32[]{:S(2)}, u32[]{:S(2)}) collective-permute-start(f32[2,72,640]{2,1,0:T(8,128)S(1)} %pad_maximum_fusion.2.refs_3_), channel_id=1, source_target_pairs={{0,1},{1,0},{2,3},{3,2},{4,5},{5,4},{6,7},{7,6},{8,9},{9,8},{10,11... | collective-permute-start | bytes 1105928 | tf_op jit(solution)/shard_map/ppermute | solution.py:32
  42.5 7.4 %collective-permute-done.6 = f32[72,640]{1,0:T(8,128)S(1)} collective-permute-done((f32[72,640]{1,0:T(8,128)S(1)}, f32[72,640]{1,0:T(8,128)S(1)}, u32[]{:S(2)}, u32[]{:S(2)}) %collective-permute-start.6) | collective-permute-done | bytes 184352 | tf_op jit(solution)/shard_map/ppermute | solution.py:32
  49.9 0.9 collective-permute-start.11
  50.9 0.9 collective-permute-done.11.refs_9_
  51.9 0.7 copy-done.20
  52.5 11.9 %shard_map.103 = (f32[3,384,640]{2,1,0:T(8,128)}, f32[640,1152]{1,0:T(8,128)}) custom-call(s32[16]{0:T(128)S(1)} %pad_add_fusion.1.owner_ref, f32[1,72,640]{2,1,0:T(8,128)} %bitcast.43, f32[2,72,640]{2,1,0:T(8,128)} %copy-done.13, f32[2,72,640]{2,1,0:T(8,128)} %copy-done.14, f32[2,72,640]{2,1,0:T(8,128)} %copy-done.15, f32[1,72,640]{2,1,0:T(8,128)} %bitcast.55, ...), custom_call_target="tpu_custom_call" | custom-call | flops 3963617280 | bytes 1024 | tf_op jit(solution)/shard_map/pallas_call | solution.py:311
  64.4 6.6 %all-to-all-start.1 = ((f32[16,40,1152]{2,1,0:T(8,128)}), f32[16,40,1152]{2,1,0:T(8,128)}, u32[]{:S(2)}, u32[]{:S(2)}) async-start(f32[16,40,1152]{2,1,0:T(8,128)} %bitcast.48), calls=%async_computation.1 | async-start | bytes 5898240 | tf_op jit(solution)/shard_map/all_to_all | solution.py:395
  71.1 10.9 %shard_map.105 = (f32[8,72,640]{2,1,0:T(8,128)}, f32[8,72,640]{2,1,0:T(8,128)}) custom-call(s32[16]{0:T(128)S(1)} %pad_add_fusion.2.owner_ref, f32[16,72,640]{2,1,0:T(8,128)S(1)} %all-to-all-done.lower_hbm, f32[2,384,384]{2,1,0:T(8,128)} %lower_ref.1, f32[640,640]{1,0:T(8,128)} %anc_hbm.1), custom_call_target="tpu_custom_call" | custom-call | flops 3963617280 | bytes 1024 | tf_op jit(solution)/shard_map/pallas_call | solution.py:311
  82.0 0.7 collective-permute-start.12
  82.8 1.4 copy-done.9
  84.1 2.5 %shard_map.106.ends_ref = f32[168,24]{1,0:T(8,128)S(1)} custom-call(s32[2]{0:T(128)S(1)} %pad_add_fusion.place_ref._, f32[8,72,640]{2,1,0:T(8,128)S(1)} %copy-done.9, f32[2,384,384]{2,1,0:T(8,128)S(1)} %copy-done.11, f32[2,384,384]{2,1,0:T(8,128)S(1)} %copy-done.10, f32[3,384,384]{2,1,0:T(8,128)S(1)} %copy-done.8), custom_call_target="tpu_custom_call" | custom-call | flops 396361728000 | bytes 1024 | tf_op jit(solution)/shard_map/pallas_call | solution.py:311
  86.7 1.6 %add_bitcast_fusion.1 = (f32[72,640]{1,0:T(8,128)S(1)}, f32[72,640]{1,0:T(8,128)S(1)}, f32[72,640]{1,0:T(8,128)S(1)}, f32[72,640]{1,0:T(8,128)S(1)}, f32[72,640]...) fusion(f32[8,72,640]{2,1,0:T(8,128)} %collective-permute-done.12, f32[8,72,640]{2,1,0:T(8,128)S(1)} %copy-done.12), kind=kLoop, calls=%fused_computation.6 | loop fusion | flops 322560 | bytes 3870720 | tf_op jit(solution)/shard_map/add | solution.py:52
  88.4 2.7 %collective-permute-start.17 = (f32[72,640]{1,0:T(8,128)S(1)}, f32[72,640]{1,0:T(8,128)S(1)}, u32[]{:S(2)}, u32[]{:S(2)}) collective-permute-start(f32[72,640]{1,0:T(8,128)S(1)} %get-tuple-element.55), channel_id=1, source_target_pairs={{0,14},{1,15},{2,0},{3,1},{4,2},{5,3},{6,4},{7,5},{8,6},{9,7},{10,... | collective-permute-start | bytes 552968 | tf_op jit(solution)/shard_map/ppermute | solution.py:32
  91.0 4.9 %collective-permute-done.13 = f32[72,640]{1,0:T(8,128)S(1)} collective-permute-done((f32[72,640]{1,0:T(8,128)S(1)}, f32[72,640]{1,0:T(8,128)S(1)}, u32[]{:S(2)}, u32[]{:S(2)}) %collective-permute-start.13) | collective-permute-done | bytes 184352 | tf_op jit(solution)/shard_map/ppermute | solution.py:32
  95.9 1.0 bitcast_add_fusion
  97.2 2.7 %collective-permute-start.18 = (f32[72,640]{1,0:T(8,128)S(1)}, f32[72,640]{1,0:T(8,128)S(1)}, u32[]{:S(2)}, u32[]{:S(2)}) collective-permute-start(f32[72,640]{1,0:T(8,128)S(1)} %add.176), channel_id=1, source_target_pairs={{0,14},{1,15},{2,0},{3,1},{4,2},{5,3},{6,4},{7,5},{8,6},{9,7},{10,... | collective-permute-start | bytes 552968 | tf_op jit(solution)/shard_map/ppermute | solution.py:32
  100.0 4.0 %collective-permute-done.14 = f32[72,640]{1,0:T(8,128)S(1)} collective-permute-done((f32[72,640]{1,0:T(8,128)S(1)}, f32[72,640]{1,0:T(8,128)S(1)}, u32[]{:S(2)}, u32[]{:S(2)}) %collective-permute-start.14) | collective-permute-done | bytes 184352 | tf_op jit(solution)/shard_map/ppermute | solution.py:32
  104.1 2.7 %collective-permute-start.19 = (f32[72,640]{1,0:T(8,128)S(1)}, f32[72,640]{1,0:T(8,128)S(1)}, u32[]{:S(2)}, u32[]{:S(2)}) collective-permute-start(f32[72,640]{1,0:T(8,128)S(1)} %add.177), channel_id=1, source_target_pairs={{0,14},{1,15},{2,0},{3,1},{4,2},{5,3},{6,4},{7,5},{8,6},{9,7},{10,... | collective-permute-start | bytes 552968 | tf_op jit(solution)/shard_map/ppermute | solution.py:32
  106.8 3.2 %collective-permute-done.15 = f32[72,640]{1,0:T(8,128)S(1)} collective-permute-done((f32[72,640]{1,0:T(8,128)S(1)}, f32[72,640]{1,0:T(8,128)S(1)}, u32[]{:S(2)}, u32[]{:S(2)}) %collective-permute-start.15) | collective-permute-done | bytes 184352 | tf_op jit(solution)/shard_map/ppermute | solution.py:32
  110.1 0.7 add.172
  110.8 5.9 %collective-permute-done.16 = f32[72,640]{1,0:T(8,128)} collective-permute-done((f32[72,640]{1,0:T(8,128)}, f32[72,640]{1,0:T(8,128)}, u32[]{:S(2)}, u32[]{:S(2)}) %collective-permute-start.16) | collective-permute-done | bytes 184352 | tf_op jit(solution)/shard_map/ppermute | solution.py:32
  116.7 1.0 add_add_fusion.cols_ref
  117.7 1.9 %shard_map.107 = (f32[16,72,72]{2,1,0:T(8,128)S(1)}, f32[16,40,72]{2,1,0:T(8,128)S(1)}) custom-call(s32[16]{0:T(128)S(1)} %fusion.owner_ref, f32[3,384,640]{2,1,0:T(8,128)S(1)} %copy-done, f32[72,640]{1,0:T(8,128)S(1)} %add_add_fusion.cols_ref), custom_call_target="tpu_custom_call" | custom-call | flops 318504960 | bytes 1024 | tf_op jit(solution)/shard_map/pallas_call | solution.py:311
  119.6 0.7 copy-done.2
  120.3 2.6 %collective-permute-start.21 = (f32[4,72,72]{2,1,0:T(8,128)S(1)}, f32[4,72,72]{2,1,0:T(8,128)S(1)}, u32[]{:S(2)}, u32[]{:S(2)}) collective-permute-start(f32[4,72,72]{2,1,0:T(8,128)S(1)} %get-tuple-element.61), channel_id=1, source_target_pairs={{0,128},{16,144},{32,160},{48,176},{64,192},{80,208},{96,224},{112... | collective-permute-start | bytes 248840 | tf_op jit(solution)/shard_map/ppermute | solution.py:27
  122.9 1.5 collective-permute-start.22
  124.4 8.0 %all-to-all-start.2 = ((f32[16,40,72]{2,1,0:T(8,128)}), f32[16,40,72]{2,1,0:T(8,128)S(1)}, u32[]{:S(2)}, u32[]{:S(2)}) async-start(f32[16,40,72]{2,1,0:T(8,128)} %copy-done.2), calls=%async_computation.2 | async-start | bytes 655360 | tf_op jit(solution)/shard_map/all_to_all | solution.py:416
  132.5 2.6 %collective-permute-start.25 = (f32[72,72]{1,0:T(8,128)S(1)}, f32[72,72]{1,0:T(8,128)S(1)}, u32[]{:S(2)}, u32[]{:S(2)}) collective-permute-start(f32[72,72]{1,0:T(8,128)S(1)} %get-tuple-element.64), channel_id=1, source_target_pairs={{0,48},{16,0},{32,16},{48,32},{64,112},{80,64},{96,80},{112,96},{1... | collective-permute-start | bytes 62216 | tf_op jit(solution)/shard_map/ppermute | solution.py:27
  135.1 0.6 collective-permute-start.24
  135.7 0.4 collective-permute-start.23
  136.2 3.2 %shard_map.109 = f32[3,40,384]{2,1,0:T(8,128)} custom-call(s32[2]{0:T(128)S(1)} %pad_add_fusion.place_ref._, f32[16,40,1152]{2,1,0:T(8,128)} %all-to-all-done.1.got_hbm), custom_call_target="tpu_custom_call" | custom-call | flops 1000 | bytes 1024 | tf_op jit(solution)/shard_map/pallas_call | solution.py:311
  140.1 5.3 %all-to-all-done.2.got_ref = f32[16,40,72]{2,1,0:T(8,128)S(1)} async-done(((f32[16,40,72]{2,1,0:T(8,128)}), f32[16,40,72]{2,1,0:T(8,128)S(1)}, u32[]{:S(2)}, u32[]{:S(2)}) %all-to-all-start.2) | async-done | bytes 184352 | tf_op jit(solution)/shard_map/all_to_all | solution.py:416
  145.5 1.6 %shard_map.108 = (f32[3,24,24]{2,1,0:T(8,128)}, f32[2,2,24,24]{3,2,1,0:T(8,128)}, f32[3,40,384]{2,1,0:T(8,128)}) custom-call(s32[2]{0:T(128)S(1)} %pad_add_fusion.place_ref._, f32[72,72]{1,0:T(8,128)S(1)} %get-tuple-element.67.a_ref, f32[72,72]{1,0:T(8,128)S(1)} %collective-permute-done.23.b_ref, f32[72,72]{1,0:T(8,128)S(1)} %collective-permute-done.24.c_ref, ...), custom_call_target="tpu_custom_call" | custom-call | bytes 1024 | tf_op jit(solution)/shard_map/pallas_call | solution.py:311
  (79 shorter events, 2.5 us)
Async XLA Ops:
  0.7 0.9 copy-start.3
  3.0 23.1 %copy-start.1 = (f32[72,640]{1,0:T(8,128)}, f32[72,640]{1,0:T(8,128)S(1)}, u32[]{:S(2)}) copy-start(f32[72,640]{1,0:T(8,128)S(1)} %shard_map.102._) | copy-start | bytes 552964
  3.1 1.0 copy-start.4
  6.5 58.0 %all-to-all-start = ((f32[16,72,640]{2,1,0:T(8,128)}), f32[16,72,640]{2,1,0:T(8,128)S(1)}, u32[]{:S(2)}, u32[]{:S(2)}) async-start(f32[16,72,640]{2,1,0:T(8,128)} %shard_map.104), calls=%async_computation | async-start | bytes 5898240 | tf_op jit(solution)/shard_map/all_to_all | solution.py:351
  14.1 8.6 %collective-permute-start.1 = (f32[72,640]{1,0:T(8,128)S(1)}, f32[72,640]{1,0:T(8,128)S(1)}, u32[]{:S(2)}, u32[]{:S(2)}) collective-permute-start(f32[72,640]{1,0:T(8,128)S(1)} %shard_map.102._), channel_id=1, source_target_pairs={{0,14},{1,15},{2,0},{3,1},{4,2},{5,3},{6,4},{7,5},{8,6},{9,7},{10,... | collective-permute-start | bytes 552968 | tf_op jit(solution)/shard_map/ppermute | solution.py:32
  19.7 6.4 %collective-permute-start = (f32[72,640]{1,0:T(8,128)S(1)}, f32[72,640]{1,0:T(8,128)}, u32[]{:S(2)}, u32[]{:S(2)}) collective-permute-start(f32[72,640]{1,0:T(8,128)S(1)} %shard_map.102._), channel_id=1, source_target_pairs={{0,2},{1,3},{2,4},{3,5},{4,6},{5,7},{6,8},{7,9},{8,10},{9,11},{10,... | collective-permute-start | bytes 552968 | tf_op jit(solution)/shard_map/ppermute | solution.py:32
  22.7 5.9 %collective-permute-start.3 = (f32[72,640]{1,0:T(8,128)S(1)}, f32[72,640]{1,0:T(8,128)S(1)}, u32[]{:S(2)}, u32[]{:S(2)}) collective-permute-start(f32[72,640]{1,0:T(8,128)S(1)} %collective-permute-done.1), channel_id=1, source_target_pairs={{0,14},{1,15},{2,0},{3,1},{4,2},{5,3},{6,4},{7,5},{8,6},{9,7},{10,... | collective-permute-start | bytes 552968 | tf_op jit(solution)/shard_map/ppermute | solution.py:32
  26.1 6.1 %collective-permute-start.2 = (f32[72,640]{1,0:T(8,128)}, f32[72,640]{1,0:T(8,128)}, u32[]{:S(2)}, u32[]{:S(2)}) collective-permute-start(f32[72,640]{1,0:T(8,128)} %collective-permute-done), channel_id=1, source_target_pairs={{0,2},{1,3},{2,4},{3,5},{4,6},{5,7},{6,8},{7,9},{8,10},{9,11},{10,... | collective-permute-start | bytes 552968 | tf_op jit(solution)/shard_map/ppermute | solution.py:32
  26.1 24.7 %collective-permute-start.7 = (f32[1,72,640]{2,1,0:T(8,128)S(1)}, f32[1,72,640]{2,1,0:T(8,128)}, u32[]{:S(2)}, u32[]{:S(2)}) collective-permute-start(f32[1,72,640]{2,1,0:T(8,128)S(1)} %bitcast.42), channel_id=1, source_target_pairs={{0,1},{1,0},{2,3},{3,2},{4,5},{5,4},{6,7},{7,6},{8,9},{9,8},{10,11... | collective-permute-start | bytes 552968 | tf_op jit(solution)/shard_map/ppermute | solution.py:32
  28.6 8.9 %collective-permute-start.5 = (f32[72,640]{1,0:T(8,128)S(1)}, f32[72,640]{1,0:T(8,128)S(1)}, u32[]{:S(2)}, u32[]{:S(2)}) collective-permute-start(f32[72,640]{1,0:T(8,128)S(1)} %collective-permute-done.3), channel_id=1, source_target_pairs={{0,14},{1,15},{2,0},{3,1},{4,2},{5,3},{6,4},{7,5},{8,6},{9,7},{10,... | collective-permute-start | bytes 552968 | tf_op jit(solution)/shard_map/ppermute | solution.py:32
  32.2 6.1 %collective-permute-start.4 = (f32[72,640]{1,0:T(8,128)}, f32[72,640]{1,0:T(8,128)S(1)}, u32[]{:S(2)}, u32[]{:S(2)}) collective-permute-start(f32[72,640]{1,0:T(8,128)} %collective-permute-done.2), channel_id=1, source_target_pairs={{0,2},{1,3},{2,4},{3,5},{4,6},{5,7},{6,8},{7,9},{8,10},{9,11},{10,... | collective-permute-start | bytes 552968 | tf_op jit(solution)/shard_map/ppermute | solution.py:32
  33.2 18.6 %copy-start.13 = (f32[2,72,640]{2,1,0:T(8,128)}, f32[2,72,640]{2,1,0:T(8,128)S(1)}, u32[]{:S(2)}) copy-start(f32[2,72,640]{2,1,0:T(8,128)S(1)} %pad_maximum_fusion.refs_1_) | copy-start | bytes 1105924
  33.2 17.7 %collective-permute-start.8 = (f32[2,72,640]{2,1,0:T(8,128)S(1)}, f32[2,72,640]{2,1,0:T(8,128)S(1)}, u32[]{:S(2)}, u32[]{:S(2)}) collective-permute-start(f32[2,72,640]{2,1,0:T(8,128)S(1)} %pad_maximum_fusion.refs_1_), channel_id=1, source_target_pairs={{0,1},{1,0},{2,3},{3,2},{4,5},{5,4},{6,7},{7,6},{8,9},{9,8},{10,11... | collective-permute-start | bytes 1105928 | tf_op jit(solution)/shard_map/ppermute | solution.py:32
  37.3 14.4 %copy-start.14 = (f32[2,72,640]{2,1,0:T(8,128)}, f32[2,72,640]{2,1,0:T(8,128)S(1)}, u32[]{:S(2)}) copy-start(f32[2,72,640]{2,1,0:T(8,128)S(1)} %pad_maximum_fusion.1.refs_2_) | copy-start | bytes 1105924
  37.3 13.5 %collective-permute-start.9 = (f32[2,72,640]{2,1,0:T(8,128)S(1)}, f32[2,72,640]{2,1,0:T(8,128)S(1)}, u32[]{:S(2)}, u32[]{:S(2)}) collective-permute-start(f32[2,72,640]{2,1,0:T(8,128)S(1)} %pad_maximum_fusion.1.refs_2_), channel_id=1, source_target_pairs={{0,1},{1,0},{2,3},{3,2},{4,5},{5,4},{6,7},{7,6},{8,9},{9,8},{10,11... | collective-permute-start | bytes 1105928 | tf_op jit(solution)/shard_map/ppermute | solution.py:32
  38.4 13.4 %copy-start.15 = (f32[2,72,640]{2,1,0:T(8,128)}, f32[2,72,640]{2,1,0:T(8,128)S(1)}, u32[]{:S(2)}) copy-start(f32[2,72,640]{2,1,0:T(8,128)S(1)} %pad_maximum_fusion.2.refs_3_) | copy-start | bytes 1105924
  38.4 12.5 %collective-permute-start.10 = (f32[2,72,640]{2,1,0:T(8,128)S(1)}, f32[2,72,640]{2,1,0:T(8,128)S(1)}, u32[]{:S(2)}, u32[]{:S(2)}) collective-permute-start(f32[2,72,640]{2,1,0:T(8,128)S(1)} %pad_maximum_fusion.2.refs_3_), channel_id=1, source_target_pairs={{0,1},{1,0},{2,3},{3,2},{4,5},{5,4},{6,7},{7,6},{8,9},{9,8},{10,11... | collective-permute-start | bytes 1105928 | tf_op jit(solution)/shard_map/ppermute | solution.py:32
  42.4 7.4 %collective-permute-start.6 = (f32[72,640]{1,0:T(8,128)S(1)}, f32[72,640]{1,0:T(8,128)S(1)}, u32[]{:S(2)}, u32[]{:S(2)}) collective-permute-start(f32[72,640]{1,0:T(8,128)S(1)} %collective-permute-done.4), channel_id=1, source_target_pairs={{0,2},{1,3},{2,4},{3,5},{4,6},{5,7},{6,8},{7,9},{8,10},{9,11},{10,... | collective-permute-start | bytes 552968 | tf_op jit(solution)/shard_map/ppermute | solution.py:32
  49.8 1.9 %copy-start.19 = (f32[72,640]{1,0:T(8,128)}, f32[72,640]{1,0:T(8,128)S(1)}, u32[]{:S(2)}) copy-start(f32[72,640]{1,0:T(8,128)S(1)} %collective-permute-done.6) | copy-start | bytes 552964
  49.9 1.9 %collective-permute-start.11 = (f32[1,72,640]{2,1,0:T(8,128)S(1)}, f32[1,72,640]{2,1,0:T(8,128)S(1)}, u32[]{:S(2)}, u32[]{:S(2)}) collective-permute-start(f32[1,72,640]{2,1,0:T(8,128)S(1)} %bitcast.54), channel_id=1, source_target_pairs={{0,1},{1,0},{2,3},{3,2},{4,5},{5,4},{6,7},{7,6},{8,9},{9,8},{10,11... | collective-permute-start | bytes 552968 | tf_op jit(solution)/shard_map/ppermute | solution.py:32
  50.9 0.9 copy-start.16
  50.9 0.9 copy-start.17
  50.9 1.0 copy-start.18
  64.4 55.9 %all-to-all-start.1 = ((f32[16,40,1152]{2,1,0:T(8,128)}), f32[16,40,1152]{2,1,0:T(8,128)}, u32[]{:S(2)}, u32[]{:S(2)}) async-start(f32[16,40,1152]{2,1,0:T(8,128)} %bitcast.48), calls=%async_computation.1 | async-start | bytes 5898240 | tf_op jit(solution)/shard_map/all_to_all | solution.py:395
  71.1 11.7 %copy-start.8 = (f32[3,384,384]{2,1,0:T(8,128)S(1)}, f32[3,384,384]{2,1,0:T(8,128)}, u32[]{:S(2)}) copy-start(f32[3,384,384]{2,1,0:T(8,128)} %diag_ref.1) | copy-start | bytes 5308420
  71.1 11.7 %copy-start.10 = (f32[2,384,384]{2,1,0:T(8,128)S(1)}, f32[2,384,384]{2,1,0:T(8,128)}, u32[]{:S(2)}) copy-start(f32[2,384,384]{2,1,0:T(8,128)} %upper_ref.1) | copy-start | bytes 3538948
  71.1 11.7 %copy-start.11 = (f32[2,384,384]{2,1,0:T(8,128)S(1)}, f32[2,384,384]{2,1,0:T(8,128)}, u32[]{:S(2)}) copy-start(f32[2,384,384]{2,1,0:T(8,128)} %lower_ref.1) | copy-start | bytes 3538948
  82.0 4.6 %collective-permute-start.12 = (f32[8,72,640]{2,1,0:T(8,128)}, f32[8,72,640]{2,1,0:T(8,128)}, u32[]{:S(2)}, u32[]{:S(2)}) collective-permute-start(f32[8,72,640]{2,1,0:T(8,128)} %get-tuple-element.33._), channel_id=1, source_target_pairs={{0,1},{1,0},{2,3},{3,2},{4,5},{5,4},{6,7},{7,6},{8,9},{9,8},{10,11... | collective-permute-start | bytes 4423688 | tf_op jit(solution)/shard_map/ppermute | solution.py:32
  82.8 1.4 copy-start.9
  84.1 2.6 %copy-start.12 = (f32[8,72,640]{2,1,0:T(8,128)S(1)}, f32[8,72,640]{2,1,0:T(8,128)}, u32[]{:S(2)}) copy-start(f32[8,72,640]{2,1,0:T(8,128)} %get-tuple-element.32) | copy-start | bytes 4423684
  86.7 1.6 %copy-start.5 = (f32[168,24]{1,0:T(8,128)}, f32[168,24]{1,0:T(8,128)S(1)}, u32[]{:S(2)}) copy-start(f32[168,24]{1,0:T(8,128)S(1)} %shard_map.106.ends_ref) | copy-start | bytes 48388
  88.3 7.6 %collective-permute-start.13 = (f32[72,640]{1,0:T(8,128)S(1)}, f32[72,640]{1,0:T(8,128)S(1)}, u32[]{:S(2)}, u32[]{:S(2)}) collective-permute-start(f32[72,640]{1,0:T(8,128)S(1)} %get-tuple-element.54), channel_id=1, source_target_pairs={{0,2},{1,3},{2,4},{3,5},{4,6},{5,7},{6,8},{7,9},{8,10},{9,11},{10,... | collective-permute-start | bytes 552968 | tf_op jit(solution)/shard_map/ppermute | solution.py:32
  88.4 8.8 %collective-permute-start.17 = (f32[72,640]{1,0:T(8,128)S(1)}, f32[72,640]{1,0:T(8,128)S(1)}, u32[]{:S(2)}, u32[]{:S(2)}) collective-permute-start(f32[72,640]{1,0:T(8,128)S(1)} %get-tuple-element.55), channel_id=1, source_target_pairs={{0,14},{1,15},{2,0},{3,1},{4,2},{5,3},{6,4},{7,5},{8,6},{9,7},{10,... | collective-permute-start | bytes 552968 | tf_op jit(solution)/shard_map/ppermute | solution.py:32
  96.9 7.1 %collective-permute-start.14 = (f32[72,640]{1,0:T(8,128)S(1)}, f32[72,640]{1,0:T(8,128)S(1)}, u32[]{:S(2)}, u32[]{:S(2)}) collective-permute-start(f32[72,640]{1,0:T(8,128)S(1)} %bitcast_add_fusion), channel_id=1, source_target_pairs={{0,2},{1,3},{2,4},{3,5},{4,6},{5,7},{6,8},{7,9},{8,10},{9,11},{10,... | collective-permute-start | bytes 552968 | tf_op jit(solution)/shard_map/ppermute | solution.py:32
  97.2 20.5 %copy-start = (f32[3,384,640]{2,1,0:T(8,128)S(1)}, f32[3,384,640]{2,1,0:T(8,128)}, u32[]{:S(2)}) copy-start(f32[3,384,640]{2,1,0:T(8,128)} %get-tuple-element.29.upper_ref) | copy-start | bytes 8847364
  97.2 6.8 %collective-permute-start.18 = (f32[72,640]{1,0:T(8,128)S(1)}, f32[72,640]{1,0:T(8,128)S(1)}, u32[]{:S(2)}, u32[]{:S(2)}) collective-permute-start(f32[72,640]{1,0:T(8,128)S(1)} %add.176), channel_id=1, source_target_pairs={{0,14},{1,15},{2,0},{3,1},{4,2},{5,3},{6,4},{7,5},{8,6},{9,7},{10,... | collective-permute-start | bytes 552968 | tf_op jit(solution)/shard_map/ppermute | solution.py:32
  104.0 6.1 %collective-permute-start.15 = (f32[72,640]{1,0:T(8,128)S(1)}, f32[72,640]{1,0:T(8,128)S(1)}, u32[]{:S(2)}, u32[]{:S(2)}) collective-permute-start(f32[72,640]{1,0:T(8,128)S(1)} %add.171), channel_id=1, source_target_pairs={{0,2},{1,3},{2,4},{3,5},{4,6},{5,7},{6,8},{7,9},{8,10},{9,11},{10,... | collective-permute-start | bytes 552968 | tf_op jit(solution)/shard_map/ppermute | solution.py:32
  104.1 6.7 %collective-permute-start.19 = (f32[72,640]{1,0:T(8,128)S(1)}, f32[72,640]{1,0:T(8,128)S(1)}, u32[]{:S(2)}, u32[]{:S(2)}) collective-permute-start(f32[72,640]{1,0:T(8,128)S(1)} %add.177), channel_id=1, source_target_pairs={{0,14},{1,15},{2,0},{3,1},{4,2},{5,3},{6,4},{7,5},{8,6},{9,7},{10,... | collective-permute-start | bytes 552968 | tf_op jit(solution)/shard_map/ppermute | solution.py:32
  110.8 5.9 %collective-permute-start.16 = (f32[72,640]{1,0:T(8,128)}, f32[72,640]{1,0:T(8,128)}, u32[]{:S(2)}, u32[]{:S(2)}) collective-permute-start(f32[72,640]{1,0:T(8,128)} %add.172), channel_id=1, source_target_pairs={{0,2},{1,3},{2,4},{3,5},{4,6},{5,7},{6,8},{7,9},{8,10},{9,11},{10,... | collective-permute-start | bytes 552968 | tf_op jit(solution)/shard_map/ppermute | solution.py:32
  119.6 0.7 copy-start.2
  120.3 12.1 %collective-permute-start.21 = (f32[4,72,72]{2,1,0:T(8,128)S(1)}, f32[4,72,72]{2,1,0:T(8,128)S(1)}, u32[]{:S(2)}, u32[]{:S(2)}) collective-permute-start(f32[4,72,72]{2,1,0:T(8,128)S(1)} %get-tuple-element.61), channel_id=1, source_target_pairs={{0,128},{16,144},{32,160},{48,176},{64,192},{80,208},{96,224},{112... | collective-permute-start | bytes 248840 | tf_op jit(solution)/shard_map/ppermute | solution.py:27
  122.9 9.5 %collective-permute-start.22 = (f32[4,72,72]{2,1,0:T(8,128)S(1)}, f32[4,72,72]{2,1,0:T(8,128)S(1)}, u32[]{:S(2)}, u32[]{:S(2)}) collective-permute-start(f32[4,72,72]{2,1,0:T(8,128)S(1)} %get-tuple-element.62), channel_id=1, source_target_pairs={{0,192},{16,208},{32,224},{48,240},{64,0},{80,16},{96,32},{112,48}... | collective-permute-start | bytes 248840 | tf_op jit(solution)/shard_map/ppermute | solution.py:27
  124.4 8.0 %collective-permute-start.20 = (f32[4,72,72]{2,1,0:T(8,128)S(1)}, f32[4,72,72]{2,1,0:T(8,128)S(1)}, u32[]{:S(2)}, u32[]{:S(2)}) collective-permute-start(f32[4,72,72]{2,1,0:T(8,128)S(1)} %get-tuple-element.63), channel_id=1, source_target_pairs={{0,64},{16,80},{32,96},{48,112},{64,128},{80,144},{96,160},{112,17... | collective-permute-start | bytes 248840 | tf_op jit(solution)/shard_map/ppermute | solution.py:27
  124.4 21.1 %all-to-all-start.2 = ((f32[16,40,72]{2,1,0:T(8,128)}), f32[16,40,72]{2,1,0:T(8,128)S(1)}, u32[]{:S(2)}, u32[]{:S(2)}) async-start(f32[16,40,72]{2,1,0:T(8,128)} %copy-done.2), calls=%async_computation.2 | async-start | bytes 655360 | tf_op jit(solution)/shard_map/all_to_all | solution.py:416
  132.5 6.8 %collective-permute-start.25 = (f32[72,72]{1,0:T(8,128)S(1)}, f32[72,72]{1,0:T(8,128)S(1)}, u32[]{:S(2)}, u32[]{:S(2)}) collective-permute-start(f32[72,72]{1,0:T(8,128)S(1)} %get-tuple-element.64), channel_id=1, source_target_pairs={{0,48},{16,0},{32,16},{48,32},{64,112},{80,64},{96,80},{112,96},{1... | collective-permute-start | bytes 62216 | tf_op jit(solution)/shard_map/ppermute | solution.py:27
  135.1 4.6 %collective-permute-start.24 = (f32[72,72]{1,0:T(8,128)S(1)}, f32[72,72]{1,0:T(8,128)S(1)}, u32[]{:S(2)}, u32[]{:S(2)}) collective-permute-start(f32[72,72]{1,0:T(8,128)S(1)} %get-tuple-element.65), channel_id=1, source_target_pairs={{0,32},{16,48},{32,0},{48,16},{64,96},{80,112},{96,64},{112,80},{1... | collective-permute-start | bytes 62216 | tf_op jit(solution)/shard_map/ppermute | solution.py:27
  135.7 9.8 %copy-start.6 = (f32[168,24]{1,0:T(8,128)S(1)}, f32[168,24]{1,0:T(8,128)}, u32[]{:S(2)}) copy-start(f32[168,24]{1,0:T(8,128)} %copy-done.5) | copy-start | bytes 48388
  135.7 4.4 %collective-permute-start.23 = (f32[72,72]{1,0:T(8,128)S(1)}, f32[72,72]{1,0:T(8,128)S(1)}, u32[]{:S(2)}, u32[]{:S(2)}) collective-permute-start(f32[72,72]{1,0:T(8,128)S(1)} %get-tuple-element.66), channel_id=1, source_target_pairs={{0,16},{16,32},{32,48},{48,0},{64,80},{80,96},{96,112},{112,64},{1... | collective-permute-start | bytes 62216 | tf_op jit(solution)/shard_map/ppermute | solution.py:27
  (2 other events, 1.4 us)

commit v2 on v1

--- a/solution.py
+++ b/solution.py
@@ -40,7 +40,7 @@
     for _ in range(3):
         up.append(to_col(up[-1], 1, 0))
         down.append(to_col(down[-1], -1, 0))
-    far = to_col(up[3], 1, 0)
+    far = jnp.concatenate([to_col(up[3][:40], 1, 0), to_col(down[3][40:], -1, 0)], axis=0)
     blocks = [value[None]]
     for t in range(1, 4):
         blocks.append(jnp.stack([up[t], down[t]]))

time: 148 us -> 146 us (0.986)
  waiting for transfers between devices: 36.7 us -> 32.1 us
  starting transfers between devices: 62.2 us -> 64.4 us
    ppermute x20 -> x21, waiting for transfers between devices: 30.5 us -> 25.9 us  [to_col(): return lax.ppermute(value, 'col', pairs)]
    ppermute x20 -> x21, starting transfers between devices: 32.2 us -> 34.5 us  [to_col(): return lax.ppermute(value, 'col', pairs)]
    unnamed x42 -> x44, local copies, waits for them, and re-layouts: 5.5 us -> 6.12 us
  transfers between devices with their start and end apart: 29 -> 30, of which waited for: 13 -> 12; matrix products, arithmetic and copies ran while one was open for 4% -> 4% of each run, Pallas kernels for 21% -> 21%
where the time goes in v2:
time: 146 us; the launch traced here: 145 us
  starting transfers between devices  64.4 us (44%)
  Pallas kernels  35.1 us (24%)
  waiting for transfers between devices  32.1 us (22%)
  other arithmetic  6.56 us (4%)
  local copies, waits for them, and re-layouts  6.18 us (4%)
    pallas_call x8, Pallas kernels, call(): pl.pallas_call(kernel, out_shape=[pltpu.HBM(o, jnp.float32) if space == '...  35.1 us
    ppermute x21, starting transfers between devices, to_col(): return lax.ppermute(value, 'col', pairs)  34.5 us
    ppermute x21, waiting for transfers between devices, to_col(): return lax.ppermute(value, 'col', pairs)  25.9 us
    all_to_all x1, starting transfers between devices, per_device(): got = lax.all_to_all(sent, 'col', 0, 0)  8.05 us
    ppermute x6, starting transfers between devices, to_row(): return lax.ppermute(value, 'row', pairs)  7.68 us
    all_to_all x1, starting transfers between devices, per_device(): lower_all = lax.all_to_all(lower_all, 'row', 0, 0)  7.6 us
    all_to_all x1, starting transfers between devices, per_device(): rows_got = lax.all_to_all(rows_part, 'row', 0, 0)  6.63 us
    unnamed x44, local copies, waits for them, and re-layouts  6.12 us
  transfers between devices with their start and end apart: 30, of which 12 were waited for; matrix products, arithmetic and copies ran while one was open for 4% of the time, Pallas kernels for 21%

profile of v2, /device:TPU:1, one launch (start us, length us, event | category | flops | bytes accessed | tf_op | source)
XLA Modules:
  0.0 145.4 jit_solution(15658051343980956399)
XLA Ops:
  0.7 0.9 copy-done.3
  1.6 0.7 copy-done.7
  2.3 0.7 shard_map.102._
  3.1 1.0 copy-done.4
  4.0 2.4 %shard_map.104 = f32[16,72,640]{2,1,0:T(8,128)} custom-call(s32[2]{0:T(128)S(1)} %pad_add_fusion.place_ref._, s32[3,3,80]{2,1,0:T(4,128)S(1)} %bitcast.48, f32[72,640]{1,0:T(8,128)S(1)} %shard_map.102._, f32[3,24,640]{2,1,0:T(8,128)S(1)} %bitcast.46), custom_call_target="tpu_custom_call" | custom-call | flops 1000 | bytes 1024 | tf_op jit(solution)/shard_map/pallas_call | solution.py:311
  6.5 7.6 %all-to-all-start = ((f32[16,72,640]{2,1,0:T(8,128)}), f32[16,72,640]{2,1,0:T(8,128)S(1)}, u32[]{:S(2)}, u32[]{:S(2)}) async-start(f32[16,72,640]{2,1,0:T(8,128)} %shard_map.104), calls=%async_computation | async-start | bytes 5898240 | tf_op jit(solution)/shard_map/all_to_all | solution.py:351
  14.1 5.7 %collective-permute-start.1 = (f32[72,640]{1,0:T(8,128)S(1)}, f32[72,640]{1,0:T(8,128)S(1)}, u32[]{:S(2)}, u32[]{:S(2)}) collective-permute-start(f32[72,640]{1,0:T(8,128)S(1)} %shard_map.102._), channel_id=1, source_target_pairs={{0,14},{1,15},{2,0},{3,1},{4,2},{5,3},{6,4},{7,5},{8,6},{9,7},{10,... | collective-permute-start | bytes 552968 | tf_op jit(solution)/shard_map/ppermute | solution.py:32
  19.7 3.0 %collective-permute-done.1 = f32[72,640]{1,0:T(8,128)S(1)} collective-permute-done((f32[72,640]{1,0:T(8,128)S(1)}, f32[72,640]{1,0:T(8,128)S(1)}, u32[]{:S(2)}, u32[]{:S(2)}) %collective-permute-start.1) | collective-permute-done | bytes 184352 | tf_op jit(solution)/shard_map/ppermute | solution.py:32
  22.7 3.4 %collective-permute-start.3 = (f32[72,640]{1,0:T(8,128)S(1)}, f32[72,640]{1,0:T(8,128)}, u32[]{:S(2)}, u32[]{:S(2)}) collective-permute-start(f32[72,640]{1,0:T(8,128)S(1)} %collective-permute-done.1), channel_id=1, source_target_pairs={{0,14},{1,15},{2,0},{3,1},{4,2},{5,3},{6,4},{7,5},{8,6},{9,7},{10,... | collective-permute-start | bytes 552968 | tf_op jit(solution)/shard_map/ppermute | solution.py:32
  26.1 2.5 %collective-permute-done.3 = f32[72,640]{1,0:T(8,128)} collective-permute-done((f32[72,640]{1,0:T(8,128)S(1)}, f32[72,640]{1,0:T(8,128)}, u32[]{:S(2)}, u32[]{:S(2)}) %collective-permute-start.3) | collective-permute-done | bytes 184352 | tf_op jit(solution)/shard_map/ppermute | solution.py:32
  28.6 3.4 %collective-permute-start.5 = (f32[72,640]{1,0:T(8,128)}, f32[72,640]{1,0:T(8,128)S(1)}, u32[]{:S(2)}, u32[]{:S(2)}) collective-permute-start(f32[72,640]{1,0:T(8,128)} %collective-permute-done.3), channel_id=1, source_target_pairs={{0,14},{1,15},{2,0},{3,1},{4,2},{5,3},{6,4},{7,5},{8,6},{9,7},{10,... | collective-permute-start | bytes 552968 | tf_op jit(solution)/shard_map/ppermute | solution.py:32
  32.2 0.9 pad_maximum_fusion.refs_1_
  33.2 3.1 %collective-permute-start.9 = (f32[2,72,640]{2,1,0:T(8,128)S(1)}, f32[2,72,640]{2,1,0:T(8,128)S(1)}, u32[]{:S(2)}, u32[]{:S(2)}) collective-permute-start(f32[2,72,640]{2,1,0:T(8,128)S(1)} %pad_maximum_fusion.refs_1_), channel_id=1, source_target_pairs={{0,1},{1,0},{2,3},{3,2},{4,5},{5,4},{6,7},{7,6},{8,9},{9,8},{10,11... | collective-permute-start | bytes 1105928 | tf_op jit(solution)/shard_map/ppermute | solution.py:32
  36.3 0.9 pad_maximum_fusion.1.refs_2_
  37.4 3.0 %collective-permute-start.7 = (f32[32,640]{1,0:T(8,128)S(1)}, f32[32,640]{1,0:T(8,128)S(1)}, u32[]{:S(2)}, u32[]{:S(2)}) collective-permute-start(f32[32,640]{1,0:T(8,128)S(1)} %slice.109), channel_id=1, source_target_pairs={{0,14},{1,15},{2,0},{3,1},{4,2},{5,3},{6,4},{7,5},{8,6},{9,7},{10,... | collective-permute-start | bytes 245768 | tf_op jit(solution)/shard_map/ppermute | solution.py:32
  40.6 1.8 %collective-permute-start.11 = (f32[2,72,640]{2,1,0:T(8,128)S(1)}, f32[2,72,640]{2,1,0:T(8,128)S(1)}, u32[]{:S(2)}, u32[]{:S(2)}) collective-permute-start(f32[2,72,640]{2,1,0:T(8,128)S(1)} %pad_maximum_fusion.2.refs_3_), channel_id=1, source_target_pairs={{0,1},{1,0},{2,3},{3,2},{4,5},{5,4},{6,7},{7,6},{8,9},{9,8},{10,11... | collective-permute-start | bytes 1105928 | tf_op jit(solution)/shard_map/ppermute | solution.py:32
  42.4 1.8 %collective-permute-start.8 = (f32[1,72,640]{2,1,0:T(8,128)S(1)}, f32[1,72,640]{2,1,0:T(8,128)S(1)}, u32[]{:S(2)}, u32[]{:S(2)}) collective-permute-start(f32[1,72,640]{2,1,0:T(8,128)S(1)} %bitcast.43), channel_id=1, source_target_pairs={{0,1},{1,0},{2,3},{3,2},{4,5},{5,4},{6,7},{7,6},{8,9},{9,8},{10,11... | collective-permute-start | bytes 552968 | tf_op jit(solution)/shard_map/ppermute | solution.py:32
  44.1 1.4 collective-permute-done.6
  45.5 2.8 %collective-permute-start.12 = (f32[1,72,640]{2,1,0:T(8,128)S(1)}, f32[1,72,640]{2,1,0:T(8,128)S(1)}, u32[]{:S(2)}, u32[]{:S(2)}) collective-permute-start(f32[1,72,640]{2,1,0:T(8,128)S(1)} %maximum_bitcast_fusion.refs_4_), channel_id=1, source_target_pairs={{0,1},{1,0},{2,3},{3,2},{4,5},{5,4},{6,7},{7,6},{8,9},{9,8},{10,11... | collective-permute-start | bytes 552968 | tf_op jit(solution)/shard_map/ppermute | solution.py:32
  48.5 0.9 collective-permute-done.12.refs_9_
  49.5 0.6 copy-done.21
  50.1 0.7 copy-done.19
  50.8 11.9 %shard_map.103 = (f32[3,384,640]{2,1,0:T(8,128)}, f32[640,1152]{1,0:T(8,128)}) custom-call(s32[16]{0:T(128)S(1)} %pad_add_fusion.1.owner_ref, f32[1,72,640]{2,1,0:T(8,128)} %bitcast.44, f32[2,72,640]{2,1,0:T(8,128)} %copy-done.13, f32[2,72,640]{2,1,0:T(8,128)} %copy-done.14, f32[2,72,640]{2,1,0:T(8,128)} %copy-done.15, f32[1,72,640]{2,1,0:T(8,128)} %copy-done.16, ...), custom_call_target="tpu_custom_call" | custom-call | flops 3963617280 | bytes 1024 | tf_op jit(solution)/shard_map/pallas_call | solution.py:311
  62.7 6.6 %all-to-all-start.1 = ((f32[16,40,1152]{2,1,0:T(8,128)}), f32[16,40,1152]{2,1,0:T(8,128)}, u32[]{:S(2)}, u32[]{:S(2)}) async-start(f32[16,40,1152]{2,1,0:T(8,128)} %bitcast.49), calls=%async_computation.1 | async-start | bytes 5898240 | tf_op jit(solution)/shard_map/all_to_all | solution.py:395
  69.3 10.9 %shard_map.105 = (f32[8,72,640]{2,1,0:T(8,128)}, f32[8,72,640]{2,1,0:T(8,128)}) custom-call(s32[16]{0:T(128)S(1)} %pad_add_fusion.2.owner_ref, f32[16,72,640]{2,1,0:T(8,128)S(1)} %all-to-all-done.lower_hbm, f32[2,384,384]{2,1,0:T(8,128)} %lower_ref.1, f32[640,640]{1,0:T(8,128)} %anc_hbm.1), custom_call_target="tpu_custom_call" | custom-call | flops 3963617280 | bytes 1024 | tf_op jit(solution)/shard_map/pallas_call | solution.py:311
  80.3 0.7 collective-permute-start.13
  81.0 1.4 copy-done.9
  82.4 2.5 %shard_map.106.ends_ref = f32[168,24]{1,0:T(8,128)S(1)} custom-call(s32[2]{0:T(128)S(1)} %pad_add_fusion.place_ref._, f32[8,72,640]{2,1,0:T(8,128)S(1)} %copy-done.9, f32[2,384,384]{2,1,0:T(8,128)S(1)} %copy-done.11, f32[2,384,384]{2,1,0:T(8,128)S(1)} %copy-done.10, f32[3,384,384]{2,1,0:T(8,128)S(1)} %copy-done.8), custom_call_target="tpu_custom_call" | custom-call | flops 396361728000 | bytes 1024 | tf_op jit(solution)/shard_map/pallas_call | solution.py:311
  85.0 1.6 %add_bitcast_fusion.1 = (f32[72,640]{1,0:T(8,128)S(1)}, f32[72,640]{1,0:T(8,128)S(1)}, f32[72,640]{1,0:T(8,128)S(1)}, f32[72,640]{1,0:T(8,128)S(1)}, f32[72,640]...) fusion(f32[8,72,640]{2,1,0:T(8,128)} %collective-permute-done.13, f32[8,72,640]{2,1,0:T(8,128)S(1)} %copy-done.12), kind=kLoop, calls=%fused_computation.7 | loop fusion | flops 322560 | bytes 3870720 | tf_op jit(solution)/shard_map/add | solution.py:52
  86.7 2.7 %collective-permute-start.18 = (f32[72,640]{1,0:T(8,128)S(1)}, f32[72,640]{1,0:T(8,128)S(1)}, u32[]{:S(2)}, u32[]{:S(2)}) collective-permute-start(f32[72,640]{1,0:T(8,128)S(1)} %get-tuple-element.55), channel_id=1, source_target_pairs={{0,14},{1,15},{2,0},{3,1},{4,2},{5,3},{6,4},{7,5},{8,6},{9,7},{10,... | collective-permute-start | bytes 552968 | tf_op jit(solution)/shard_map/ppermute | solution.py:32
  89.3 4.9 %collective-permute-done.14 = f32[72,640]{1,0:T(8,128)S(1)} collective-permute-done((f32[72,640]{1,0:T(8,128)S(1)}, f32[72,640]{1,0:T(8,128)S(1)}, u32[]{:S(2)}, u32[]{:S(2)}) %collective-permute-start.14) | collective-permute-done | bytes 184352 | tf_op jit(solution)/shard_map/ppermute | solution.py:32
  94.2 1.0 bitcast_add_fusion
  95.5 2.7 %collective-permute-start.19 = (f32[72,640]{1,0:T(8,128)S(1)}, f32[72,640]{1,0:T(8,128)S(1)}, u32[]{:S(2)}, u32[]{:S(2)}) collective-permute-start(f32[72,640]{1,0:T(8,128)S(1)} %add.176), channel_id=1, source_target_pairs={{0,14},{1,15},{2,0},{3,1},{4,2},{5,3},{6,4},{7,5},{8,6},{9,7},{10,... | collective-permute-start | bytes 552968 | tf_op jit(solution)/shard_map/ppermute | solution.py:32
  98.2 4.0 %collective-permute-done.15 = f32[72,640]{1,0:T(8,128)S(1)} collective-permute-done((f32[72,640]{1,0:T(8,128)S(1)}, f32[72,640]{1,0:T(8,128)S(1)}, u32[]{:S(2)}, u32[]{:S(2)}) %collective-permute-start.15) | collective-permute-done | bytes 184352 | tf_op jit(solution)/shard_map/ppermute | solution.py:32
  102.4 2.7 %collective-permute-start.20 = (f32[72,640]{1,0:T(8,128)S(1)}, f32[72,640]{1,0:T(8,128)S(1)}, u32[]{:S(2)}, u32[]{:S(2)}) collective-permute-start(f32[72,640]{1,0:T(8,128)S(1)} %add.177), channel_id=1, source_target_pairs={{0,14},{1,15},{2,0},{3,1},{4,2},{5,3},{6,4},{7,5},{8,6},{9,7},{10,... | collective-permute-start | bytes 552968 | tf_op jit(solution)/shard_map/ppermute | solution.py:32
  105.1 3.2 %collective-permute-done.16 = f32[72,640]{1,0:T(8,128)S(1)} collective-permute-done((f32[72,640]{1,0:T(8,128)S(1)}, f32[72,640]{1,0:T(8,128)S(1)}, u32[]{:S(2)}, u32[]{:S(2)}) %collective-permute-start.16) | collective-permute-done | bytes 184352 | tf_op jit(solution)/shard_map/ppermute | solution.py:32
  108.3 0.7 add.172
  109.1 5.9 %collective-permute-done.17 = f32[72,640]{1,0:T(8,128)} collective-permute-done((f32[72,640]{1,0:T(8,128)}, f32[72,640]{1,0:T(8,128)}, u32[]{:S(2)}, u32[]{:S(2)}) %collective-permute-start.17) | collective-permute-done | bytes 184352 | tf_op jit(solution)/shard_map/ppermute | solution.py:32
  114.9 1.0 add_add_fusion.cols_ref
  115.9 1.9 %shard_map.107 = (f32[16,72,72]{2,1,0:T(8,128)S(1)}, f32[16,40,72]{2,1,0:T(8,128)S(1)}) custom-call(s32[16]{0:T(128)S(1)} %fusion.owner_ref, f32[3,384,640]{2,1,0:T(8,128)S(1)} %copy-done, f32[72,640]{1,0:T(8,128)S(1)} %add_add_fusion.cols_ref), custom_call_target="tpu_custom_call" | custom-call | flops 318504960 | bytes 1024 | tf_op jit(solution)/shard_map/pallas_call | solution.py:311
  117.9 0.7 copy-done.2
  118.6 2.6 %collective-permute-start.22 = (f32[4,72,72]{2,1,0:T(8,128)S(1)}, f32[4,72,72]{2,1,0:T(8,128)S(1)}, u32[]{:S(2)}, u32[]{:S(2)}) collective-permute-start(f32[4,72,72]{2,1,0:T(8,128)S(1)} %get-tuple-element.61), channel_id=1, source_target_pairs={{0,128},{16,144},{32,160},{48,176},{64,192},{80,208},{96,224},{112... | collective-permute-start | bytes 248840 | tf_op jit(solution)/shard_map/ppermute | solution.py:27
  121.2 1.5 %collective-permute-start.23 = (f32[4,72,72]{2,1,0:T(8,128)S(1)}, f32[4,72,72]{2,1,0:T(8,128)S(1)}, u32[]{:S(2)}, u32[]{:S(2)}) collective-permute-start(f32[4,72,72]{2,1,0:T(8,128)S(1)} %get-tuple-element.62), channel_id=1, source_target_pairs={{0,192},{16,208},{32,224},{48,240},{64,0},{80,16},{96,32},{112,48}... | collective-permute-start | bytes 248840 | tf_op jit(solution)/shard_map/ppermute | solution.py:27
  122.7 8.0 %all-to-all-start.2 = ((f32[16,40,72]{2,1,0:T(8,128)}), f32[16,40,72]{2,1,0:T(8,128)S(1)}, u32[]{:S(2)}, u32[]{:S(2)}) async-start(f32[16,40,72]{2,1,0:T(8,128)} %copy-done.2), calls=%async_computation.2 | async-start | bytes 655360 | tf_op jit(solution)/shard_map/all_to_all | solution.py:416
  130.8 2.6 %collective-permute-start.26 = (f32[72,72]{1,0:T(8,128)S(1)}, f32[72,72]{1,0:T(8,128)S(1)}, u32[]{:S(2)}, u32[]{:S(2)}) collective-permute-start(f32[72,72]{1,0:T(8,128)S(1)} %get-tuple-element.64), channel_id=1, source_target_pairs={{0,48},{16,0},{32,16},{48,32},{64,112},{80,64},{96,80},{112,96},{1... | collective-permute-start | bytes 62216 | tf_op jit(solution)/shard_map/ppermute | solution.py:27
  134.5 3.2 %shard_map.109 = f32[3,40,384]{2,1,0:T(8,128)} custom-call(s32[2]{0:T(128)S(1)} %pad_add_fusion.place_ref._, f32[16,40,1152]{2,1,0:T(8,128)} %all-to-all-done.1.got_hbm), custom_call_target="tpu_custom_call" | custom-call | flops 1000 | bytes 1024 | tf_op jit(solution)/shard_map/pallas_call | solution.py:311
  138.4 5.4 %all-to-all-done.2.got_ref = f32[16,40,72]{2,1,0:T(8,128)S(1)} async-done(((f32[16,40,72]{2,1,0:T(8,128)}), f32[16,40,72]{2,1,0:T(8,128)S(1)}, u32[]{:S(2)}, u32[]{:S(2)}) %all-to-all-start.2) | async-done | bytes 184352 | tf_op jit(solution)/shard_map/all_to_all | solution.py:416
  143.8 1.6 %shard_map.108 = (f32[3,24,24]{2,1,0:T(8,128)}, f32[2,2,24,24]{3,2,1,0:T(8,128)}, f32[3,40,384]{2,1,0:T(8,128)}) custom-call(s32[2]{0:T(128)S(1)} %pad_add_fusion.place_ref._, f32[72,72]{1,0:T(8,128)S(1)} %get-tuple-element.67.a_ref, f32[72,72]{1,0:T(8,128)S(1)} %collective-permute-done.24.b_ref, f32[72,72]{1,0:T(8,128)S(1)} %collective-permute-done.25.c_ref, ...), custom_call_target="tpu_custom_call" | custom-call | bytes 1024 | tf_op jit(solution)/shard_map/pallas_call | solution.py:311
  (86 shorter events, 3.4 us)
Async XLA Ops:
  0.7 0.9 copy-start.3
  3.0 39.3 %copy-start.1 = (f32[72,640]{1,0:T(8,128)}, f32[72,640]{1,0:T(8,128)S(1)}, u32[]{:S(2)}) copy-start(f32[72,640]{1,0:T(8,128)S(1)} %shard_map.102._) | copy-start | bytes 552964
  3.1 1.0 copy-start.4
  6.5 56.2 %all-to-all-start = ((f32[16,72,640]{2,1,0:T(8,128)}), f32[16,72,640]{2,1,0:T(8,128)S(1)}, u32[]{:S(2)}, u32[]{:S(2)}) async-start(f32[16,72,640]{2,1,0:T(8,128)} %shard_map.104), calls=%async_computation | async-start | bytes 5898240 | tf_op jit(solution)/shard_map/all_to_all | solution.py:351
  14.1 8.6 %collective-permute-start.1 = (f32[72,640]{1,0:T(8,128)S(1)}, f32[72,640]{1,0:T(8,128)S(1)}, u32[]{:S(2)}, u32[]{:S(2)}) collective-permute-start(f32[72,640]{1,0:T(8,128)S(1)} %shard_map.102._), channel_id=1, source_target_pairs={{0,14},{1,15},{2,0},{3,1},{4,2},{5,3},{6,4},{7,5},{8,6},{9,7},{10,... | collective-permute-start | bytes 552968 | tf_op jit(solution)/shard_map/ppermute | solution.py:32
  19.7 6.4 %collective-permute-start = (f32[72,640]{1,0:T(8,128)S(1)}, f32[72,640]{1,0:T(8,128)}, u32[]{:S(2)}, u32[]{:S(2)}) collective-permute-start(f32[72,640]{1,0:T(8,128)S(1)} %shard_map.102._), channel_id=1, source_target_pairs={{0,2},{1,3},{2,4},{3,5},{4,6},{5,7},{6,8},{7,9},{8,10},{9,11},{10,... | collective-permute-start | bytes 552968 | tf_op jit(solution)/shard_map/ppermute | solution.py:32
  22.7 5.9 %collective-permute-start.3 = (f32[72,640]{1,0:T(8,128)S(1)}, f32[72,640]{1,0:T(8,128)}, u32[]{:S(2)}, u32[]{:S(2)}) collective-permute-start(f32[72,640]{1,0:T(8,128)S(1)} %collective-permute-done.1), channel_id=1, source_target_pairs={{0,14},{1,15},{2,0},{3,1},{4,2},{5,3},{6,4},{7,5},{8,6},{9,7},{10,... | collective-permute-start | bytes 552968 | tf_op jit(solution)/shard_map/ppermute | solution.py:32
  26.1 6.1 %collective-permute-start.2 = (f32[72,640]{1,0:T(8,128)}, f32[72,640]{1,0:T(8,128)S(1)}, u32[]{:S(2)}, u32[]{:S(2)}) collective-permute-start(f32[72,640]{1,0:T(8,128)} %collective-permute-done), channel_id=1, source_target_pairs={{0,2},{1,3},{2,4},{3,5},{4,6},{5,7},{6,8},{7,9},{8,10},{9,11},{10,... | collective-permute-start | bytes 552968 | tf_op jit(solution)/shard_map/ppermute | solution.py:32
  28.6 8.8 %collective-permute-start.5 = (f32[72,640]{1,0:T(8,128)}, f32[72,640]{1,0:T(8,128)S(1)}, u32[]{:S(2)}, u32[]{:S(2)}) collective-permute-start(f32[72,640]{1,0:T(8,128)} %collective-permute-done.3), channel_id=1, source_target_pairs={{0,14},{1,15},{2,0},{3,1},{4,2},{5,3},{6,4},{7,5},{8,6},{9,7},{10,... | collective-permute-start | bytes 552968 | tf_op jit(solution)/shard_map/ppermute | solution.py:32
  32.2 8.2 %collective-permute-start.4 = (f32[72,640]{1,0:T(8,128)S(1)}, f32[72,640]{1,0:T(8,128)S(1)}, u32[]{:S(2)}, u32[]{:S(2)}) collective-permute-start(f32[72,640]{1,0:T(8,128)S(1)} %collective-permute-done.2), channel_id=1, source_target_pairs={{0,2},{1,3},{2,4},{3,5},{4,6},{5,7},{6,8},{7,9},{8,10},{9,11},{10,... | collective-permute-start | bytes 552968 | tf_op jit(solution)/shard_map/ppermute | solution.py:32
  33.2 16.2 %copy-start.13 = (f32[2,72,640]{2,1,0:T(8,128)}, f32[2,72,640]{2,1,0:T(8,128)S(1)}, u32[]{:S(2)}) copy-start(f32[2,72,640]{2,1,0:T(8,128)S(1)} %pad_maximum_fusion.refs_1_) | copy-start | bytes 1105924
  33.2 15.3 %collective-permute-start.9 = (f32[2,72,640]{2,1,0:T(8,128)S(1)}, f32[2,72,640]{2,1,0:T(8,128)S(1)}, u32[]{:S(2)}, u32[]{:S(2)}) collective-permute-start(f32[2,72,640]{2,1,0:T(8,128)S(1)} %pad_maximum_fusion.refs_1_), channel_id=1, source_target_pairs={{0,1},{1,0},{2,3},{3,2},{4,5},{5,4},{6,7},{7,6},{8,9},{9,8},{10,11... | collective-permute-start | bytes 1105928 | tf_op jit(solution)/shard_map/ppermute | solution.py:32
  37.2 12.2 %copy-start.14 = (f32[2,72,640]{2,1,0:T(8,128)}, f32[2,72,640]{2,1,0:T(8,128)S(1)}, u32[]{:S(2)}) copy-start(f32[2,72,640]{2,1,0:T(8,128)S(1)} %pad_maximum_fusion.1.refs_2_) | copy-start | bytes 1105924
  37.2 11.3 %collective-permute-start.10 = (f32[2,72,640]{2,1,0:T(8,128)S(1)}, f32[2,72,640]{2,1,0:T(8,128)S(1)}, u32[]{:S(2)}, u32[]{:S(2)}) collective-permute-start(f32[2,72,640]{2,1,0:T(8,128)S(1)} %pad_maximum_fusion.1.refs_2_), channel_id=1, source_target_pairs={{0,1},{1,0},{2,3},{3,2},{4,5},{5,4},{6,7},{7,6},{8,9},{9,8},{10,11... | collective-permute-start | bytes 1105928 | tf_op jit(solution)/shard_map/ppermute | solution.py:32
  37.4 5.0 %collective-permute-start.7 = (f32[32,640]{1,0:T(8,128)S(1)}, f32[32,640]{1,0:T(8,128)S(1)}, u32[]{:S(2)}, u32[]{:S(2)}) collective-permute-start(f32[32,640]{1,0:T(8,128)S(1)} %slice.109), channel_id=1, source_target_pairs={{0,14},{1,15},{2,0},{3,1},{4,2},{5,3},{6,4},{7,5},{8,6},{9,7},{10,... | collective-permute-start | bytes 245768 | tf_op jit(solution)/shard_map/ppermute | solution.py:32
  40.4 5.1 %collective-permute-start.6 = (f32[40,640]{1,0:T(8,128)S(1)}, f32[40,640]{1,0:T(8,128)S(1)}, u32[]{:S(2)}, u32[]{:S(2)}) collective-permute-start(f32[40,640]{1,0:T(8,128)S(1)} %slice.108), channel_id=1, source_target_pairs={{0,2},{1,3},{2,4},{3,5},{4,6},{5,7},{6,8},{7,9},{8,10},{9,11},{10,... | collective-permute-start | bytes 307208 | tf_op jit(solution)/shard_map/ppermute | solution.py:32
  40.6 8.8 %copy-start.15 = (f32[2,72,640]{2,1,0:T(8,128)}, f32[2,72,640]{2,1,0:T(8,128)S(1)}, u32[]{:S(2)}) copy-start(f32[2,72,640]{2,1,0:T(8,128)S(1)} %pad_maximum_fusion.2.refs_3_) | copy-start | bytes 1105924
  40.6 8.8 %collective-permute-start.11 = (f32[2,72,640]{2,1,0:T(8,128)S(1)}, f32[2,72,640]{2,1,0:T(8,128)S(1)}, u32[]{:S(2)}, u32[]{:S(2)}) collective-permute-start(f32[2,72,640]{2,1,0:T(8,128)S(1)} %pad_maximum_fusion.2.refs_3_), channel_id=1, source_target_pairs={{0,1},{1,0},{2,3},{3,2},{4,5},{5,4},{6,7},{7,6},{8,9},{9,8},{10,11... | collective-permute-start | bytes 1105928 | tf_op jit(solution)/shard_map/ppermute | solution.py:32
  42.4 6.1 %collective-permute-start.8 = (f32[1,72,640]{2,1,0:T(8,128)S(1)}, f32[1,72,640]{2,1,0:T(8,128)S(1)}, u32[]{:S(2)}, u32[]{:S(2)}) collective-permute-start(f32[1,72,640]{2,1,0:T(8,128)S(1)} %bitcast.43), channel_id=1, source_target_pairs={{0,1},{1,0},{2,3},{3,2},{4,5},{5,4},{6,7},{7,6},{8,9},{9,8},{10,11... | collective-permute-start | bytes 552968 | tf_op jit(solution)/shard_map/ppermute | solution.py:32
  45.5 3.9 %copy-start.16 = (f32[1,72,640]{2,1,0:T(8,128)}, f32[1,72,640]{2,1,0:T(8,128)S(1)}, u32[]{:S(2)}) copy-start(f32[1,72,640]{2,1,0:T(8,128)S(1)} %maximum_bitcast_fusion.refs_4_) | copy-start | bytes 552964
  45.5 3.8 %collective-permute-start.12 = (f32[1,72,640]{2,1,0:T(8,128)S(1)}, f32[1,72,640]{2,1,0:T(8,128)S(1)}, u32[]{:S(2)}, u32[]{:S(2)}) collective-permute-start(f32[1,72,640]{2,1,0:T(8,128)S(1)} %maximum_bitcast_fusion.refs_4_), channel_id=1, source_target_pairs={{0,1},{1,0},{2,3},{3,2},{4,5},{5,4},{6,7},{7,6},{8,9},{9,8},{10,11... | collective-permute-start | bytes 552968 | tf_op jit(solution)/shard_map/ppermute | solution.py:32
  48.5 0.9 copy-start.20
  48.5 0.9 copy-start.17
  48.5 0.9 copy-start.18
  62.7 55.9 %all-to-all-start.1 = ((f32[16,40,1152]{2,1,0:T(8,128)}), f32[16,40,1152]{2,1,0:T(8,128)}, u32[]{:S(2)}, u32[]{:S(2)}) async-start(f32[16,40,1152]{2,1,0:T(8,128)} %bitcast.49), calls=%async_computation.1 | async-start | bytes 5898240 | tf_op jit(solution)/shard_map/all_to_all | solution.py:395
  69.3 11.7 %copy-start.8 = (f32[3,384,384]{2,1,0:T(8,128)S(1)}, f32[3,384,384]{2,1,0:T(8,128)}, u32[]{:S(2)}) copy-start(f32[3,384,384]{2,1,0:T(8,128)} %diag_ref.1) | copy-start | bytes 5308420
  69.3 11.7 %copy-start.10 = (f32[2,384,384]{2,1,0:T(8,128)S(1)}, f32[2,384,384]{2,1,0:T(8,128)}, u32[]{:S(2)}) copy-start(f32[2,384,384]{2,1,0:T(8,128)} %upper_ref.1) | copy-start | bytes 3538948
  69.3 11.7 %copy-start.11 = (f32[2,384,384]{2,1,0:T(8,128)S(1)}, f32[2,384,384]{2,1,0:T(8,128)}, u32[]{:S(2)}) copy-start(f32[2,384,384]{2,1,0:T(8,128)} %lower_ref.1) | copy-start | bytes 3538948
  80.3 4.7 %collective-permute-start.13 = (f32[8,72,640]{2,1,0:T(8,128)}, f32[8,72,640]{2,1,0:T(8,128)}, u32[]{:S(2)}, u32[]{:S(2)}) collective-permute-start(f32[8,72,640]{2,1,0:T(8,128)} %get-tuple-element.33._), channel_id=1, source_target_pairs={{0,1},{1,0},{2,3},{3,2},{4,5},{5,4},{6,7},{7,6},{8,9},{9,8},{10,11... | collective-permute-start | bytes 4423688 | tf_op jit(solution)/shard_map/ppermute | solution.py:32
  81.0 1.4 copy-start.9
  82.4 2.6 %copy-start.12 = (f32[8,72,640]{2,1,0:T(8,128)S(1)}, f32[8,72,640]{2,1,0:T(8,128)}, u32[]{:S(2)}) copy-start(f32[8,72,640]{2,1,0:T(8,128)} %get-tuple-element.32) | copy-start | bytes 4423684
  85.0 1.6 %copy-start.5 = (f32[168,24]{1,0:T(8,128)}, f32[168,24]{1,0:T(8,128)S(1)}, u32[]{:S(2)}) copy-start(f32[168,24]{1,0:T(8,128)S(1)} %shard_map.106.ends_ref) | copy-start | bytes 48388
  86.6 7.6 %collective-permute-start.14 = (f32[72,640]{1,0:T(8,128)S(1)}, f32[72,640]{1,0:T(8,128)S(1)}, u32[]{:S(2)}, u32[]{:S(2)}) collective-permute-start(f32[72,640]{1,0:T(8,128)S(1)} %get-tuple-element.54), channel_id=1, source_target_pairs={{0,2},{1,3},{2,4},{3,5},{4,6},{5,7},{6,8},{7,9},{8,10},{9,11},{10,... | collective-permute-start | bytes 552968 | tf_op jit(solution)/shard_map/ppermute | solution.py:32
  86.7 8.8 %collective-permute-start.18 = (f32[72,640]{1,0:T(8,128)S(1)}, f32[72,640]{1,0:T(8,128)S(1)}, u32[]{:S(2)}, u32[]{:S(2)}) collective-permute-start(f32[72,640]{1,0:T(8,128)S(1)} %get-tuple-element.55), channel_id=1, source_target_pairs={{0,14},{1,15},{2,0},{3,1},{4,2},{5,3},{6,4},{7,5},{8,6},{9,7},{10,... | collective-permute-start | bytes 552968 | tf_op jit(solution)/shard_map/ppermute | solution.py:32
  95.2 7.1 %collective-permute-start.15 = (f32[72,640]{1,0:T(8,128)S(1)}, f32[72,640]{1,0:T(8,128)S(1)}, u32[]{:S(2)}, u32[]{:S(2)}) collective-permute-start(f32[72,640]{1,0:T(8,128)S(1)} %bitcast_add_fusion), channel_id=1, source_target_pairs={{0,2},{1,3},{2,4},{3,5},{4,6},{5,7},{6,8},{7,9},{8,10},{9,11},{10,... | collective-permute-start | bytes 552968 | tf_op jit(solution)/shard_map/ppermute | solution.py:32
  95.5 20.5 %copy-start = (f32[3,384,640]{2,1,0:T(8,128)S(1)}, f32[3,384,640]{2,1,0:T(8,128)}, u32[]{:S(2)}) copy-start(f32[3,384,640]{2,1,0:T(8,128)} %get-tuple-element.29.upper_ref) | copy-start | bytes 8847364
  95.5 6.8 %collective-permute-start.19 = (f32[72,640]{1,0:T(8,128)S(1)}, f32[72,640]{1,0:T(8,128)S(1)}, u32[]{:S(2)}, u32[]{:S(2)}) collective-permute-start(f32[72,640]{1,0:T(8,128)S(1)} %add.176), channel_id=1, source_target_pairs={{0,14},{1,15},{2,0},{3,1},{4,2},{5,3},{6,4},{7,5},{8,6},{9,7},{10,... | collective-permute-start | bytes 552968 | tf_op jit(solution)/shard_map/ppermute | solution.py:32
  102.3 6.1 %collective-permute-start.16 = (f32[72,640]{1,0:T(8,128)S(1)}, f32[72,640]{1,0:T(8,128)S(1)}, u32[]{:S(2)}, u32[]{:S(2)}) collective-permute-start(f32[72,640]{1,0:T(8,128)S(1)} %add.171), channel_id=1, source_target_pairs={{0,2},{1,3},{2,4},{3,5},{4,6},{5,7},{6,8},{7,9},{8,10},{9,11},{10,... | collective-permute-start | bytes 552968 | tf_op jit(solution)/shard_map/ppermute | solution.py:32
  102.4 6.7 %collective-permute-start.20 = (f32[72,640]{1,0:T(8,128)S(1)}, f32[72,640]{1,0:T(8,128)S(1)}, u32[]{:S(2)}, u32[]{:S(2)}) collective-permute-start(f32[72,640]{1,0:T(8,128)S(1)} %add.177), channel_id=1, source_target_pairs={{0,14},{1,15},{2,0},{3,1},{4,2},{5,3},{6,4},{7,5},{8,6},{9,7},{10,... | collective-permute-start | bytes 552968 | tf_op jit(solution)/shard_map/ppermute | solution.py:32
  109.0 5.9 %collective-permute-start.17 = (f32[72,640]{1,0:T(8,128)}, f32[72,640]{1,0:T(8,128)}, u32[]{:S(2)}, u32[]{:S(2)}) collective-permute-start(f32[72,640]{1,0:T(8,128)} %add.172), channel_id=1, source_target_pairs={{0,2},{1,3},{2,4},{3,5},{4,6},{5,7},{6,8},{7,9},{8,10},{9,11},{10,... | collective-permute-start | bytes 552968 | tf_op jit(solution)/shard_map/ppermute | solution.py:32
  118.6 12.1 %collective-permute-start.22 = (f32[4,72,72]{2,1,0:T(8,128)S(1)}, f32[4,72,72]{2,1,0:T(8,128)S(1)}, u32[]{:S(2)}, u32[]{:S(2)}) collective-permute-start(f32[4,72,72]{2,1,0:T(8,128)S(1)} %get-tuple-element.61), channel_id=1, source_target_pairs={{0,128},{16,144},{32,160},{48,176},{64,192},{80,208},{96,224},{112... | collective-permute-start | bytes 248840 | tf_op jit(solution)/shard_map/ppermute | solution.py:27
  121.2 9.5 %collective-permute-start.23 = (f32[4,72,72]{2,1,0:T(8,128)S(1)}, f32[4,72,72]{2,1,0:T(8,128)S(1)}, u32[]{:S(2)}, u32[]{:S(2)}) collective-permute-start(f32[4,72,72]{2,1,0:T(8,128)S(1)} %get-tuple-element.62), channel_id=1, source_target_pairs={{0,192},{16,208},{32,224},{48,240},{64,0},{80,16},{96,32},{112,48}... | collective-permute-start | bytes 248840 | tf_op jit(solution)/shard_map/ppermute | solution.py:27
  122.7 8.1 %collective-permute-start.21 = (f32[4,72,72]{2,1,0:T(8,128)S(1)}, f32[4,72,72]{2,1,0:T(8,128)S(1)}, u32[]{:S(2)}, u32[]{:S(2)}) collective-permute-start(f32[4,72,72]{2,1,0:T(8,128)S(1)} %get-tuple-element.63), channel_id=1, source_target_pairs={{0,64},{16,80},{32,96},{48,112},{64,128},{80,144},{96,160},{112,17... | collective-permute-start | bytes 248840 | tf_op jit(solution)/shard_map/ppermute | solution.py:27
  122.7 21.1 %all-to-all-start.2 = ((f32[16,40,72]{2,1,0:T(8,128)}), f32[16,40,72]{2,1,0:T(8,128)S(1)}, u32[]{:S(2)}, u32[]{:S(2)}) async-start(f32[16,40,72]{2,1,0:T(8,128)} %copy-done.2), calls=%async_computation.2 | async-start | bytes 655360 | tf_op jit(solution)/shard_map/all_to_all | solution.py:416
  130.8 6.8 %collective-permute-start.26 = (f32[72,72]{1,0:T(8,128)S(1)}, f32[72,72]{1,0:T(8,128)S(1)}, u32[]{:S(2)}, u32[]{:S(2)}) collective-permute-start(f32[72,72]{1,0:T(8,128)S(1)} %get-tuple-element.64), channel_id=1, source_target_pairs={{0,48},{16,0},{32,16},{48,32},{64,112},{80,64},{96,80},{112,96},{1... | collective-permute-start | bytes 62216 | tf_op jit(solution)/shard_map/ppermute | solution.py:27
  133.4 4.6 %collective-permute-start.25 = (f32[72,72]{1,0:T(8,128)S(1)}, f32[72,72]{1,0:T(8,128)S(1)}, u32[]{:S(2)}, u32[]{:S(2)}) collective-permute-start(f32[72,72]{1,0:T(8,128)S(1)} %get-tuple-element.65), channel_id=1, source_target_pairs={{0,32},{16,48},{32,0},{48,16},{64,96},{80,112},{96,64},{112,80},{1... | collective-permute-start | bytes 62216 | tf_op jit(solution)/shard_map/ppermute | solution.py:27
  134.0 9.8 %copy-start.6 = (f32[168,24]{1,0:T(8,128)S(1)}, f32[168,24]{1,0:T(8,128)}, u32[]{:S(2)}) copy-start(f32[168,24]{1,0:T(8,128)} %copy-done.5) | copy-start | bytes 48388
  134.0 4.4 %collective-permute-start.24 = (f32[72,72]{1,0:T(8,128)S(1)}, f32[72,72]{1,0:T(8,128)S(1)}, u32[]{:S(2)}, u32[]{:S(2)}) collective-permute-start(f32[72,72]{1,0:T(8,128)S(1)} %get-tuple-element.66), channel_id=1, source_target_pairs={{0,16},{16,32},{32,48},{48,0},{64,80},{80,96},{96,112},{112,64},{1... | collective-permute-start | bytes 62216 | tf_op jit(solution)/shard_map/ppermute | solution.py:27
  (4 other events, 2.8 us)
